TPU v7x, 256 devices: a whole 4x4x8 slice. The times are simulated.
256 devices in a mesh: det: 64 (over x, z, core), head: 4 (over y).
Axes of the slice: x: 4, y: 4, z: 8, core: 2. Of those that a mesh axis runs over, the one named last changes fastest.
Arguments:
- elements: bfloat16 [32768, 1024], P('det'), may hold values from -6 to 6
- element_types: int32 [32768], P('det'), may hold values from 0 to 1, as said below
- handover_counts: int32 [64, 64], replicated, may hold values from 0 to 16, as said below
- block_lists: int32 [256, 16], P('det'), may hold values from 0 to 255, as said below
- w_first: bfloat16 [2, 1024, 2048], P(None, None, 'head'), may hold values from -0.1875 to 0.1875
- w_second: bfloat16 [2, 2048, 1024], P(None, 'head'), may hold values from -0.125 to 0.125
- w_query: bfloat16 [1024, 1024], P(None, 'head'), may hold values from -3 to 3
- key_value_weight: bfloat16 [1024, 2, 256], P(None, None, 'head'), may hold values from -0.1875 to 0.1875
- attention_cotangent: bfloat16 [32768, 1024], P('det', 'head'), may hold values from -6 to 6
Outputs:
- attended: bfloat16 [32768, 1024], P('det', 'head')
- x_grad: bfloat16 [32768, 1024], P('det', 'head')
Inputs may be any that keep to these rules, and one draw needn't show every extreme that they name: `element_types`: of the 512 elements of each device of det, exactly 256 are of each type. `handover_counts`: row d, column e counts the elements that device d of det hands to device e; every row and every column sums to 512; some entries equal 16. `block_lists`: key block k is held by device k // 4 of det; the 16 entries of a query block may repeat; the lists of the 4 query blocks of one device together name exactly 1 block, counted with repeats, held by each device of det.
All inputs are finite; a program needn't handle non-finite values.
Results may differ from a plain program's by a relative error of at most 0.024.
The roundings to bfloat16 on the way count: a program that leaves them out, or rounds other values in their place, can miss the bound.
Values may be sent and summed in bfloat16 or wider, within the bound.
A program may use at most 64 MiB of HBM per device.

v0:
```python
import jax
import jax.numpy as jnp
from jax import lax
from jax.sharding import PartitionSpec as P

HEAD_SIZE = 64
BLOCK_ROWS = 128
LISTED_COUNT = 16
GROUP_HEADS = 4


def exclusive(counts, reduce_axis):
    return jnp.cumsum(counts, axis=reduce_axis, dtype=jnp.int32) - counts


def pack_rows(source_rows, starts, amounts, capacity):
    slot_ids = jnp.arange(capacity, dtype=jnp.int32)
    row_index = jnp.clip(starts[:, None] + slot_ids[None, :], 0, source_rows.shape[0] - 1)
    usable = slot_ids[None, :] < amounts[:, None]
    picked = source_rows[row_index.reshape(-1)].reshape(
        amounts.shape[0], capacity, source_rows.shape[1]
    )
    return jnp.where(usable[:, :, None], picked, jnp.zeros_like(picked))


def unpack_rows(received, starts, amounts, total_rows):
    peer_count, capacity = (received.shape[0], received.shape[1])
    within = jnp.arange(total_rows, dtype=jnp.int32)
    end_rows = starts + amounts
    peer_ids = jnp.sum(
        (end_rows[None, :] <= within[:, None]).astype(jnp.int32), axis=1, dtype=jnp.int32
    )
    slot_ids = within - starts[peer_ids]
    flattened = received.reshape(peer_count * capacity, received.shape[2])
    return flattened[peer_ids * capacity + slot_ids]


def attend(query_block_one, cotangent_block, key_block_rows, value_block_rows):
    score_scaling = HEAD_SIZE ** (-0.5)
    score_matrix = (
        jnp.einsum(
            "oenl,iel->enoi", query_block_one, key_block_rows, preferred_element_type=jnp.float32
        )
        * score_scaling
    )
    row_max = jnp.max(score_matrix, axis=-1, keepdims=True)
    exp_scores = jnp.exp(score_matrix - row_max)
    probability = exp_scores / jnp.sum(exp_scores, axis=-1, keepdims=True)
    probability_bfloat = probability.astype(jnp.bfloat16)
    attended = jnp.einsum(
        "vnys,svx->yvnx", probability_bfloat, value_block_rows, preferred_element_type=jnp.float32
    ).astype(jnp.bfloat16)
    probability_gradient = jnp.einsum(
        "oenl,iel->enoi", cotangent_block, value_block_rows, preferred_element_type=jnp.float32
    )
    row_delta = jnp.sum(probability * probability_gradient, axis=-1, keepdims=True)
    score_gradient = (probability * (probability_gradient - row_delta)).astype(jnp.bfloat16)
    query_gradient = (
        jnp.einsum(
            "vnys,svx->yvnx", score_gradient, key_block_rows, preferred_element_type=jnp.float32
        )
        * score_scaling
    ).astype(jnp.bfloat16)
    key_gradient = (
        jnp.einsum(
            "njtw,tnjs->wns", score_gradient, query_block_one, preferred_element_type=jnp.float32
        )
        * score_scaling
    )
    value_gradient = jnp.einsum(
        "njtw,tnjs->wns", probability_bfloat, cotangent_block, preferred_element_type=jnp.float32
    )
    return (attended, query_gradient, key_gradient, value_gradient)


def shards(
    elements,
    element_types,
    handover_counts,
    block_lists,
    w_first,
    w_second,
    w_query,
    key_value_weight,
    attention_cotangent,
):
    peer_count = lax.axis_size("det")
    my_index = lax.axis_index("det")
    row_count = elements.shape[0]
    model_width = elements.shape[1]
    capacity = 2 * row_count // peer_count
    starts = exclusive(handover_counts, 1)
    offsets = exclusive(handover_counts, 0)
    send_starts = lax.dynamic_index_in_dim(starts, my_index, 0, keepdims=False)
    send_counts = lax.dynamic_index_in_dim(handover_counts, my_index, 0, keepdims=False)
    recv_starts = lax.dynamic_index_in_dim(offsets, my_index, 1, keepdims=False)
    recv_counts = lax.dynamic_index_in_dim(handover_counts, my_index, 1, keepdims=False)
    type_count = w_first.shape[0]
    per_type = row_count // type_count
    type_order = jnp.argsort(element_types, stable=True)
    back_order = (
        jnp.zeros_like(type_order).at[type_order].set(jnp.arange(row_count, dtype=jnp.int32))
    )
    sorted_rows = elements[type_order].reshape(type_count, per_type, model_width)
    preact = jnp.einsum("trd,tdh->trh", sorted_rows, w_first, preferred_element_type=jnp.float32)
    hidden = jax.nn.gelu(preact).astype(jnp.bfloat16)
    sorted_mlp = jnp.einsum("trh,thd->trd", hidden, w_second, preferred_element_type=jnp.float32)
    partial_mlp = sorted_mlp.reshape(row_count, model_width)[back_order]
    mlp_sum = lax.psum(partial_mlp, "head")
    mixed = (elements.astype(jnp.float32) + mlp_sum).astype(jnp.bfloat16)
    outbound = pack_rows(mixed, send_starts, send_counts, capacity)
    inbound = lax.all_to_all(outbound, "det", split_axis=0, concat_axis=0, tiled=True)
    moved = unpack_rows(inbound, recv_starts, recv_counts, row_count)
    kv_width = key_value_weight.shape[2]
    key_value_flat = key_value_weight.reshape(model_width, 2 * kv_width)
    query_rows_all = jnp.dot(moved, w_query, preferred_element_type=jnp.float32).astype(
        jnp.bfloat16
    )
    key_value_pairs = jnp.dot(moved, key_value_flat, preferred_element_type=jnp.float32).astype(
        jnp.bfloat16
    )
    blocks_dev = row_count // BLOCK_ROWS
    slot_count = blocks_dev * LISTED_COUNT
    per_pair = slot_count // peer_count
    flat_list = block_lists.reshape(slot_count)
    owners = flat_list // blocks_dev
    local_ids = flat_list % blocks_dev
    slot_order = jnp.arange(slot_count, dtype=jnp.int32)
    earlier = (owners[:, None] == owners[None, :]) & (slot_order[None, :] < slot_order[:, None])
    slot_rank = jnp.sum(earlier.astype(jnp.int32), axis=1, dtype=jnp.int32)
    position = owners * per_pair + slot_rank
    requests = (
        jnp.zeros((slot_count,), jnp.int32)
        .at[position]
        .set(local_ids)
        .reshape(peer_count, per_pair)
    )
    wanted = lax.all_to_all(requests, "det", split_axis=0, concat_axis=0, tiled=True)
    all_keys = lax.all_gather(key_value_pairs, "det", axis=0, tiled=True)
    listed = all_keys.reshape(-1, BLOCK_ROWS, 2 * kv_width)[flat_list]
    listed = listed.reshape(blocks_dev, LISTED_COUNT * BLOCK_ROWS, 2 * kv_width)
    kv_heads = kv_width // HEAD_SIZE
    query_block_list = query_rows_all.reshape(
        blocks_dev, BLOCK_ROWS, kv_heads, GROUP_HEADS, HEAD_SIZE
    )
    cotangent_blocks = attention_cotangent.reshape(
        blocks_dev, BLOCK_ROWS, kv_heads, GROUP_HEADS, HEAD_SIZE
    )

    def one_block(inputs):
        query_block_one, cotangent_block, key_value_rows = inputs
        key_block_rows = key_value_rows[:, :kv_width].reshape(
            LISTED_COUNT * BLOCK_ROWS, kv_heads, HEAD_SIZE
        )
        value_block_rows = key_value_rows[:, kv_width:].reshape(
            LISTED_COUNT * BLOCK_ROWS, kv_heads, HEAD_SIZE
        )
        return attend(query_block_one, cotangent_block, key_block_rows, value_block_rows)

    attended, query_gradient, key_gradient, value_gradient = lax.map(
        one_block, (query_block_list, cotangent_blocks, listed)
    )
    slot_gradients = jnp.concatenate(
        [
            key_gradient.reshape(blocks_dev, LISTED_COUNT * BLOCK_ROWS, kv_width),
            value_gradient.reshape(blocks_dev, LISTED_COUNT * BLOCK_ROWS, kv_width),
        ],
        axis=2,
    )
    slot_gradients = slot_gradients.reshape(slot_count, BLOCK_ROWS, 2 * kv_width).astype(
        jnp.bfloat16
    )
    returned = (
        jnp.zeros_like(slot_gradients)
        .at[position]
        .set(slot_gradients)
        .reshape(peer_count, per_pair, BLOCK_ROWS, 2 * kv_width)
    )
    collected = lax.all_to_all(returned, "det", split_axis=0, concat_axis=0, tiled=True)
    collected = collected.reshape(slot_count, BLOCK_ROWS, 2 * kv_width).astype(jnp.float32)
    key_gradient_total = (
        jnp.zeros((blocks_dev, BLOCK_ROWS, 2 * kv_width), jnp.float32)
        .at[wanted.reshape(-1)]
        .add(collected)
    )
    key_bfloat = key_gradient_total.reshape(row_count, 2 * kv_width).astype(jnp.bfloat16)
    contract = (((1,), (1,)), ((), ()))
    partial_back = lax.dot_general(
        query_gradient.reshape(row_count, -1), w_query, contract, preferred_element_type=jnp.float32
    )
    partial_back = partial_back + lax.dot_general(
        key_bfloat, key_value_flat, contract, preferred_element_type=jnp.float32
    )
    back_sum = lax.psum(partial_back, "head").astype(jnp.bfloat16)
    outbound_back = pack_rows(back_sum, recv_starts, recv_counts, capacity)
    inbound_back = lax.all_to_all(outbound_back, "det", split_axis=0, concat_axis=0, tiled=True)
    upstream = unpack_rows(inbound_back, send_starts, send_counts, row_count)
    sorted_up = upstream[type_order].reshape(type_count, per_type, model_width)
    hidden_grad = jnp.einsum(
        "trd,thd->trh", sorted_up, w_second, preferred_element_type=jnp.float32
    )
    preact_grad = jax.vjp(jax.nn.gelu, preact)[1](hidden_grad)[0].astype(jnp.bfloat16)
    sorted_input = jnp.einsum(
        "trh,tdh->trd", preact_grad, w_first, preferred_element_type=jnp.float32
    )
    input_part = sorted_input.reshape(row_count, model_width)[back_order]
    input_share = lax.psum_scatter(input_part, "head", scatter_dimension=1, tiled=True)
    share_width = input_share.shape[1]
    own_upstream = lax.dynamic_slice_in_dim(
        upstream, lax.axis_index("head") * share_width, share_width, 1
    )
    x_grad = (own_upstream.astype(jnp.float32) + input_share).astype(jnp.bfloat16)
    return (attended.reshape(row_count, -1), x_grad)


def solution(mesh):
    return jax.shard_map(
        shards,
        mesh=mesh,
        in_specs=(
            P("det", None),
            P("det"),
            P(),
            P("det", None),
            P(None, None, "head"),
            P(None, "head", None),
            P(None, "head"),
            P(None, None, "head"),
            P("det", "head"),
        ),
        out_specs=(P("det", "head"), P("det", "head")),
        check_vma=False,
    )
```

profile of v0, /device:TPU:1, one launch (start us, length us, event | category | flops | bytes accessed | tf_op | source)
XLA Modules:
  0.0 602.9 jit_solution(14626544373594868727)
XLA Ops:
  22.9 5.3 gather_fusion.1
  29.4 66.3 %all-reduce.3.cloned.1.call-done = f32[512,1024]{1,0:T(8,128)} async-done(((f32[512,1024]{1,0:T(8,128)}), f32[512,1024]{1,0:T(8,128)}) %all-reduce.3.cloned.1.call-update) | async-done | bytes 2097168 | tf_op jit(solution)/shard_map/psum | solution.py:109
  98.0 5.4 gather_fusion.2
  106.6 11.0 %all-to-all-start = ((bf16[64,16,1024]{2,1,0:T(8,128)(2,1)}), bf16[64,16,1024]{2,1,0:T(8,128)(2,1)}, u32[]{:S(2)}, u32[]{:S(2)}) async-start(bf16[64,16,1024]{2,1,0:T(8,128)(2,1)} %broadcast_select_fusion.1), calls=%async_computation | async-start | bytes 4194304 | tf_op jit(solution)/shard_map/all_to_all | solution.py:112
  132.9 35.3 %select_select_fusion.1 = s32[512]{0:T(512)S(1)} fusion(pred[512]{0:T(512)(128)(4,1)S(1)} %get-tuple-element.224, pred[512]{0:T(512)(128)(4,1)S(1)} %get-tuple-element.223, pred[512]{0:T(512)(128)(4,1)S(1)} %get-tuple-element.222, pred[512]{0:T(512)(128)(4,1)S(1)} %get-tuple-element.221, pred[512]{0:T(512)(128)(4,1)S(1)} %get-tuple-element.220, ...), kind=kLoop, calls=%fused_computation.250 | loop fusion | flops 29184 | bytes 33508 | tf_op jit(solution)/shard_map/gather | solution.py:33
  168.3 35.6 %select_select_fusion = s32[512]{0:T(512)S(1)} fusion(pred[512]{0:T(512)(128)(4,1)S(1)} %get-tuple-element.167, pred[512]{0:T(512)(128)(4,1)S(1)} %get-tuple-element.166, pred[512]{0:T(512)(128)(4,1)S(1)} %get-tuple-element.165, pred[512]{0:T(512)(128)(4,1)S(1)} %get-tuple-element.164, pred[512]{0:T(512)(128)(4,1)S(1)} %get-tuple-element.163, ...), kind=kLoop, calls=%fused_computation.249 | loop fusion | flops 29184 | bytes 33508 | tf_op jit(solution)/shard_map/gather | solution.py:33
  204.0 4.6 gather_fusion.3
  210.1 10.0 %scatter_custom_fusion.1 = s32[64]{0:T(128)S(1)} fusion(s32[64]{0:T(128)S(1)} %get-tuple-element.385, s32[64]{0:T(128)S(1)} %get-tuple-element.383, s32[]{:T(128)} %constant.56.clone.1), kind=kCustom, calls=%fused_computation.271 | custom fusion | bytes 260 | tf_op jit(solution)/shard_map/scatter | solution.py:135
  220.8 10.3 %all-to-all-start.1 = ((s32[64,1,1]{2,1,0:T(1,128)}), s32[64,1,1]{2,1,0:T(1,128)S(1)}, u32[]{:S(2)}, u32[]{:S(2)}) async-start(s32[64,1,1]{2,1,0:T(1,128)} %copy.91), calls=%async_computation.1 | async-start | bytes 65536 | tf_op jit(solution)/shard_map/all_to_all | solution.py:138
  237.2 55.5 %all-gather.2.cloned.1.call-done = bf16[32768,128]{1,0:T(8,128)(2,1)} async-done(((bf16[512,128]{1,0:T(8,128)(2,1)}), bf16[32768,128]{1,0:T(8,128)(2,1)}) %all-gather.2.cloned.1.call-update) | async-done | bytes 8388624 | tf_op jit(solution)/shard_map/all_gather | solution.py:139
  292.7 5.6 gather_fusion.4
  298.3 41.0 %while.16 = (s32[]{:T(128)}, bf16[4,128,1,4,64]{1,4,3,2,0:T(8,128)(2,1)}, bf16[4,128,1,4,64]{1,4,3,2,0:T(8,128)(2,1)}, bf16[4,2048,1,64]{1,3,2,0:T(8,128)(2,1)},...) while((s32[]{:T(128)}, ...), condition=%wide.region_10.11_spmd, body=%wide.region_6.10_spmd.sunk | while | flops 830700032 | bytes 62289140 | solution.py:160
  355.6 9.9 %scatter_fusion = bf16[64,128,128]{2,1,0:T(8,128)(2,1)} fusion(bf16[64,128,128]{2,1,0:T(8,128)(2,1)} %broadcast_in_dim.43, s32[64]{0:T(128)S(1)} %get-tuple-element.385, bf16[64,128,128]{2,1,0:T(8,128)(2,1)} %copy.94), kind=kCustom, calls=%fused_computation.11 | custom fusion | bytes 6291712 | tf_op jit(solution)/shard_map/scatter | solution.py:176
  365.5 6.1 %all-to-all-start.2 = ((bf16[64,1,128,128]{3,2,1,0:T(8,128)(2,1)}), bf16[64,1,128,128]{3,2,1,0:T(8,128)(2,1)}, u32[]{:S(2)}, u32[]{:S(2)}) async-start(bf16[64,1,128,128]{3,2,1,0:T(8,128)(2,1)} %bitcast.379), calls=%async_computation.2 | async-start | bytes 4194304 | tf_op jit(solution)/shard_map/all_to_all | solution.py:179
  373.4 49.4 %all-to-all-done.2 = bf16[64,1,128,128]{3,2,1,0:T(8,128)(2,1)} async-done(((bf16[64,1,128,128]{3,2,1,0:T(8,128)(2,1)}), bf16[64,1,128,128]{3,2,1,0:T(8,128)(2,1)}, u32[]{:S(2)}, u32[]{:S(2)}) %all-to-all-start.2) | async-done | bytes 2097184 | tf_op jit(solution)/shard_map/all_to_all | solution.py:179
  426.8 8.8 %scatter_fusion.1 = f32[4,128,128]{2,1,0:T(8,128)S(1)} fusion(f32[4,128,128]{2,1,0:T(8,128)S(1)} %broadcast_in_dim.42, s32[64]{0:T(128)S(1)} %fusion.73, f32[64,128,128]{2,1,0:T(8,128)} %bitcast_convert_fusion), kind=kCustom, calls=%fused_computation.12 | custom fusion | flops 1048576 | bytes 12583168 | tf_op jit(solution)/shard_map/scatter-add | solution.py:184
  438.5 42.7 %all-reduce.4 = bf16[512,1024]{1,0:T(8,128)(2,1)S(1)} all-reduce(f32[512,1024]{1,0:T(8,128)} %convolution_add_fusion), channel_id=1, replica_groups=mesh['det'=64,'head'=4] {'head'}, use_global_device_ids=true, to_apply=%region_15.16 | all-reduce | flops 524288 | bytes 3145728 | tf_op jit(solution)/shard_map/psum | solution.py:194
  481.2 5.4 gather_fusion.5
  489.8 8.0 %all-to-all-start.3 = ((bf16[64,16,1024]{2,1,0:T(8,128)(2,1)}), bf16[64,16,1024]{2,1,0:T(8,128)(2,1)}, u32[]{:S(2)}, u32[]{:S(2)}) async-start(bf16[64,16,1024]{2,1,0:T(8,128)(2,1)} %broadcast_select_fusion), calls=%async_computation.3 | async-start | bytes 4194304 | tf_op jit(solution)/shard_map/all_to_all | solution.py:196
  497.9 51.1 %all-to-all-done.3 = bf16[64,16,1024]{2,1,0:T(8,128)(2,1)} async-done(((bf16[64,16,1024]{2,1,0:T(8,128)(2,1)}), bf16[64,16,1024]{2,1,0:T(8,128)(2,1)}, u32[]{:S(2)}, u32[]{:S(2)}) %all-to-all-start.3) | async-done | bytes 2097184 | tf_op jit(solution)/shard_map/all_to_all | solution.py:196
  548.9 4.6 gather_fusion.6
  556.4 5.3 fusion.53
  561.7 5.2 gather_fusion.8
  571.1 23.1 %reduce-scatter.2.cloned.1.call-done = f32[512,256]{1,0:T(8,128)} async-done(((f32[512,1024]{1,0:T(8,128)}), f32[512,256]{1,0:T(8,128)}) %reduce-scatter.2.cloned.1.call-update) | async-done | bytes 524304 | tf_op jit(solution)/shard_map/reduce_scatter | solution.py:207
  (196 shorter events, 123.4 us)
Async XLA Ops:
  7.2 13.6 %copy-start = (bf16[2,512,1024]{2,1,0:T(8,128)(2,1)S(1)}, bf16[2,512,1024]{2,1,0:T(8,128)(2,1)}, u32[]{:S(2)}) copy-start(bf16[2,512,1024]{2,1,0:T(8,128)(2,1)} %param.16) | copy-start | bytes 6291460
  7.2 88.6 %all-reduce.3.cloned.1.call-start = ((), (), s32[]{:S(2)}) async-start(), calls=%async_computation.5 | async-start | bytes 4194304 | tf_op jit(solution)/shard_map/psum | solution.py:109
  11.8 6.6 %copy-start.13 = (s32[1024]{0:T(1024)}, s32[1024]{0:T(1024)S(1)}, u32[]{:S(2)}) copy-start(s32[1024]{0:T(1024)S(1)} %pad_clamp_fusion.4) | copy-start | bytes 12292
  14.3 8.6 %copy-start.15 = (s32[1024]{0:T(1024)}, s32[1024]{0:T(1024)S(1)}, u32[]{:S(2)}) copy-start(s32[1024]{0:T(1024)S(1)} %pad_clamp_fusion.3) | copy-start | bytes 12292
  20.7 2.2 copy-start.1
  106.6 97.4 %all-to-all-start = ((bf16[64,16,1024]{2,1,0:T(8,128)(2,1)}), bf16[64,16,1024]{2,1,0:T(8,128)(2,1)}, u32[]{:S(2)}, u32[]{:S(2)}) async-start(bf16[64,16,1024]{2,1,0:T(8,128)(2,1)} %broadcast_select_fusion.1), calls=%async_computation | async-start | bytes 4194304 | tf_op jit(solution)/shard_map/all_to_all | solution.py:112
  117.6 175.2 %all-gather.2.cloned.1.call-start = ((), (), s32[]{:S(2)}) async-start(), calls=%async_computation.6 | async-start | bytes 8519680 | tf_op jit(solution)/shard_map/all_gather | solution.py:139
  203.9 4.7 copy-start.6
  204.0 5.8 copy-start.17
  220.8 144.7 %all-to-all-start.1 = ((s32[64,1,1]{2,1,0:T(1,128)}), s32[64,1,1]{2,1,0:T(1,128)S(1)}, u32[]{:S(2)}, u32[]{:S(2)}) async-start(s32[64,1,1]{2,1,0:T(1,128)} %copy.91), calls=%async_computation.1 | async-start | bytes 65536 | tf_op jit(solution)/shard_map/all_to_all | solution.py:138
  302.6 1.3 copy-start.5
  310.7 1.3 copy-start.10
  312.9 1.3 copy-start.5
  320.9 1.3 copy-start.10
  323.1 1.3 copy-start.5
  331.2 1.3 copy-start.10
  333.4 1.3 copy-start.5
  365.5 7.6 %copy-start.12 = (bf16[4,128,1,4,64]{1,4,3,2,0:T(8,128)(2,1)S(1)}, bf16[4,128,1,4,64]{1,4,3,2,0:T(8,128)(2,1)}, u32[]{:S(2)}) copy-start(bf16[4,128,1,4,64]{1,4,3,2,0:T(8,128)(2,1)} %get-tuple-element.50) | copy-start | bytes 786436
  365.5 57.2 %all-to-all-start.2 = ((bf16[64,1,128,128]{3,2,1,0:T(8,128)(2,1)}), bf16[64,1,128,128]{3,2,1,0:T(8,128)(2,1)}, u32[]{:S(2)}, u32[]{:S(2)}) async-start(bf16[64,1,128,128]{3,2,1,0:T(8,128)(2,1)} %bitcast.379), calls=%async_computation.2 | async-start | bytes 4194304 | tf_op jit(solution)/shard_map/all_to_all | solution.py:179
  426.8 8.8 %copy-start.7 = (bf16[1024,2,64]{0,2,1:T(8,128)(2,1)S(1)}, bf16[1024,2,64]{0,2,1:T(8,128)(2,1)}, u32[]{:S(2)}) copy-start(bf16[1024,2,64]{0,2,1:T(8,128)(2,1)} %param.18) | copy-start | bytes 786436
  489.8 59.2 %all-to-all-start.3 = ((bf16[64,16,1024]{2,1,0:T(8,128)(2,1)}), bf16[64,16,1024]{2,1,0:T(8,128)(2,1)}, u32[]{:S(2)}, u32[]{:S(2)}) async-start(bf16[64,16,1024]{2,1,0:T(8,128)(2,1)} %broadcast_select_fusion), calls=%async_computation.3 | async-start | bytes 4194304 | tf_op jit(solution)/shard_map/all_to_all | solution.py:196
  497.8 96.4 %reduce-scatter.2.cloned.1.call-start = ((), (), s32[]{:S(2)}) async-start(), calls=%async_computation.7 | async-start | bytes 2621440 | tf_op jit(solution)/shard_map/reduce_scatter | solution.py:207
  548.9 4.6 copy-start.14
  556.3 5.3 copy-start.16
  (16 other events, 18.3 us)
Sparse Core Ops, SparseCore 0:
  28.3 67.4 all-reduce.2
  209.9 82.8 all-gather.1
  567.0 27.1 reduce-scatter.1
where the time goes:
time: 614 us; the launch traced here: 603 us
  waiting for transfers between devices  245 us (40%)
  other arithmetic  121 us (20%)
  local copies, waits for them, and re-layouts  103 us (17%)
  blocking collectives  42.7 us (7%)
  matrix products  40.3 us (7%)
  starting transfers between devices  35.6 us (6%)
  between operations  14.6 us (2%)
    gather x6, other arithmetic, unpack_rows(): slot_ids = within - starts[peer_ids]  80.3 us
    psum x1, waiting for transfers between devices, shards(): mlp_sum = lax.psum(partial_mlp, 'head')  66.3 us
    all_gather x1, waiting for transfers between devices, shards(): all_keys = lax.all_gather(key_value_pairs, 'det', axis=0, tiled=True)  55.5 us
    all_to_all x1, waiting for transfers between devices, shards(): lax.all_to_all(outbound_back, 'det', split_axis=0, concat_axis=0, tiled=T...  51.1 us
    all_to_all x1, waiting for transfers between devices, shards(): lax.all_to_all(returned, 'det', split_axis=0, concat_axis=0, tiled=True)  49.4 us
    psum x1, blocking collectives, shards(): back_sum = lax.psum(partial_back, 'head').astype(jnp.bfloat16)  42.7 us
    reduce_scatter x1, waiting for transfers between devices, shards(): lax.psum_scatter(input_part, 'head', scatter_dimension=1, tiled=True)  23.1 us
  transfers between devices with their start and end apart: 7, of which 5 were waited for; matrix products, arithmetic and copies ran while one was open for 30% of the time, Pallas kernels for 0%

commit v1 on v0

v1 whole, which is shorter than its diff:
```python
import functools

import jax
import jax.numpy as jnp
from jax import lax
from jax.experimental import pallas as pl
from jax.experimental.pallas import tpu as pltpu
from jax.sharding import PartitionSpec as P

HEAD_SIZE = 64
BLOCK_ROWS = 128
LISTED_COUNT = 16
GROUP_HEADS = 4
SCALE = HEAD_SIZE ** (-0.5)

F32 = jnp.float32
BF16 = jnp.bfloat16


def dot_nn(a, b):
    return lax.dot_general(a, b, (((1,), (0,)), ((), ())), preferred_element_type=F32)


def dot_nt(a, b):
    return lax.dot_general(a, b, (((1,), (1,)), ((), ())), preferred_element_type=F32)


def dot_tn(a, b):
    return lax.dot_general(a, b, (((0,), (0,)), ((), ())), preferred_element_type=F32)


def attention_kernel(
    list_ref, owner_ref, q_ref, do_ref, kv_hbm, att_ref, dq_ref, grad_ref, kv_buf, score, sems
):
    blocks = q_ref.shape[0] // BLOCK_ROWS
    rows = GROUP_HEADS * BLOCK_ROWS
    pair = 2
    steps = LISTED_COUNT // pair
    keys = pair * BLOCK_ROWS

    for b in range(blocks):

        def start(s, carry, b=b):
            slot = b * LISTED_COUNT + s
            pltpu.make_async_copy(kv_hbm.at[list_ref[slot]], kv_buf.at[slot], sems.at[b]).start()
            return carry

        lax.fori_loop(0, LISTED_COUNT, start, 0)

    def stack(ref, b):
        base = pl.multiple_of(b * BLOCK_ROWS, BLOCK_ROWS)
        tile = ref[pl.ds(base, BLOCK_ROWS), :]
        return jnp.concatenate(
            [tile[:, g * HEAD_SIZE : (g + 1) * HEAD_SIZE] for g in range(GROUP_HEADS)], axis=0
        )

    def unstack(value_t):
        parts = [
            value_t[:, g * BLOCK_ROWS : (g + 1) * BLOCK_ROWS].T for g in range(GROUP_HEADS)
        ]
        return jnp.concatenate(parts, axis=1)

    def one_block(b, carry):
        first = b * LISTED_COUNT
        pltpu.make_async_copy(
            kv_buf.at[pl.ds(first, LISTED_COUNT)], kv_buf.at[pl.ds(first, LISTED_COUNT)], sems.at[b]
        ).wait()
        q = stack(q_ref, b) * jnp.asarray(SCALE, BF16)
        do = stack(do_ref, b)
        none = jnp.zeros_like(q)
        q_pad = jnp.concatenate([q, none], axis=1)
        do_pad = jnp.concatenate([none, do], axis=1)

        def kv_at(i):
            return kv_buf[pl.ds(first + i * pair, pair)].reshape(keys, 2 * HEAD_SIZE)

        def at(i):
            return pl.ds(pl.multiple_of(i * keys, keys), keys)

        def pass_a(i, top):
            s = dot_nt(kv_at(i), q_pad)
            score[at(i), :] = s
            return jnp.maximum(top, jnp.max(s.reshape(keys // 8, 8, rows), axis=0))

        top = lax.fori_loop(0, steps, pass_a, jnp.full((8, rows), -jnp.inf, F32), unroll=2)
        top = jnp.max(top, axis=0, keepdims=True)

        def pass_b(i, carry):
            total, acc = carry
            p = jnp.exp(score[at(i), :] - top)
            score[at(i), :] = p
            total = total + jnp.sum(p.reshape(keys // 8, 8, rows), axis=0)
            acc = acc + dot_tn(kv_at(i), p.astype(BF16))
            return total, acc

        total, acc = lax.fori_loop(
            0,
            steps,
            pass_b,
            (jnp.zeros((8, rows), F32), jnp.zeros((2 * HEAD_SIZE, rows), F32)),
            unroll=2,
        )
        inverse = 1.0 / jnp.sum(total, axis=0, keepdims=True)
        out_t = acc[HEAD_SIZE:, :] * inverse
        base = pl.multiple_of(b * BLOCK_ROWS, BLOCK_ROWS)
        att_ref[pl.ds(base, BLOCK_ROWS), :] = unstack(out_t).astype(att_ref.dtype)
        delta = jnp.sum(out_t * do.astype(F32).T, axis=0, keepdims=True)
        both = jnp.concatenate([q_pad, do_pad], axis=0)

        def pass_c(i, acc):
            prob = score[at(i), :] * inverse
            kv = kv_at(i)
            dp = dot_nt(kv, do_pad)
            ds = (prob * (dp - delta)).astype(BF16)
            acc = acc + dot_tn(kv, ds)
            grads = dot_nn(jnp.concatenate([ds, prob.astype(BF16)], axis=1), both)
            grads = grads.astype(BF16)
            for k in range(pair):
                grad_ref[owner_ref[first + i * pair + k]] = grads[
                    k * BLOCK_ROWS : (k + 1) * BLOCK_ROWS
                ]
            return acc

        acc = lax.fori_loop(0, steps, pass_c, jnp.zeros((2 * HEAD_SIZE, rows), F32), unroll=2)
        dq_t = acc[:HEAD_SIZE, :] * SCALE
        dq_ref[pl.ds(base, BLOCK_ROWS), :] = unstack(dq_t).astype(dq_ref.dtype)
        return carry

    lax.fori_loop(0, blocks, one_block, 0)


def attention(lists, owners, q, do, kv):
    slots = lists.shape[0]
    vm = pl.BlockSpec(memory_space=pltpu.VMEM)
    sm = pl.BlockSpec(memory_space=pltpu.SMEM)
    return pl.pallas_call(
        attention_kernel,
        out_shape=(
            jax.ShapeDtypeStruct(q.shape, BF16),
            jax.ShapeDtypeStruct(q.shape, BF16),
            jax.ShapeDtypeStruct((slots, BLOCK_ROWS, 2 * HEAD_SIZE), BF16),
        ),
        in_specs=[sm, sm, vm, vm, pl.BlockSpec(memory_space=pl.ANY)],
        out_specs=(vm, vm, vm),
        scratch_shapes=[
            pltpu.VMEM((slots, BLOCK_ROWS, 2 * HEAD_SIZE), BF16),
            pltpu.VMEM((LISTED_COUNT * BLOCK_ROWS, GROUP_HEADS * BLOCK_ROWS), F32),
            pltpu.SemaphoreType.DMA((slots // LISTED_COUNT,)),
        ],
        compiler_params=pltpu.CompilerParams(vmem_limit_bytes=40 << 20),
        name="attention",
    )(lists, owners, q, do, kv)


def before(counts):
    ids = jnp.arange(counts.shape[0], dtype=jnp.int32)
    earlier = ids[None, :] < ids[:, None]
    return jnp.sum(jnp.where(earlier, counts[None, :], 0), axis=1, dtype=jnp.int32)


def slot_rows(counts, capacity):
    within = jnp.arange(capacity, dtype=jnp.int32)[None, :]
    rows = jnp.where(within < counts[:, None], before(counts)[:, None] + within, -1)
    return rows.reshape(-1)


def select(slot_row, row_count):
    ids = jnp.arange(row_count, dtype=jnp.int32)
    return (slot_row[:, None] == ids[None, :]).astype(BF16)


def shards(
    elements,
    element_types,
    handover_counts,
    block_lists,
    w_first,
    w_second,
    w_query,
    key_value_weight,
    attention_cotangent,
):
    peers = lax.axis_size("det")
    me = lax.axis_index("det")
    row_count, width = elements.shape
    types = w_first.shape[0]
    share = width // lax.axis_size("head")
    capacity = 2 * row_count // peers
    my_columns = lax.axis_index("head") * share

    send_rows = slot_rows(
        lax.dynamic_index_in_dim(handover_counts, me, 0, keepdims=False), capacity
    )
    recv_rows = slot_rows(
        lax.dynamic_index_in_dim(handover_counts, me, 1, keepdims=False), capacity
    )
    send_pick = select(send_rows, row_count)
    recv_pick = select(recv_rows, row_count)

    blocks = row_count // BLOCK_ROWS
    slots = blocks * LISTED_COUNT
    flat_list = block_lists.reshape(slots)
    owners = flat_list // blocks
    all_lists = lax.all_gather(flat_list, "det", axis=0, tiled=False)
    held = all_lists // blocks == me
    wanted = jnp.sum(jnp.where(held, all_lists % blocks, 0), axis=1, dtype=jnp.int32)

    mask = (element_types[:, None] == jnp.arange(types, dtype=jnp.int32)[None, :]).astype(F32)
    preact = [jnp.dot(elements, w_first[t], preferred_element_type=F32) for t in range(types)]
    partial = sum(
        jnp.dot(
            (jax.nn.gelu(preact[t]) * mask[:, t : t + 1]).astype(BF16),
            w_second[t],
            preferred_element_type=F32,
        )
        for t in range(types)
    )
    mlp = lax.psum_scatter(partial, "head", scatter_dimension=1, tiled=True)
    own = lax.dynamic_slice_in_dim(elements, my_columns, share, 1)
    mixed = (own.astype(F32) + mlp).astype(BF16)

    outbound = dot_nn(send_pick, mixed).astype(BF16).reshape(peers, capacity, share)
    inbound = lax.all_to_all(outbound, "det", split_axis=0, concat_axis=0, tiled=True)
    moved = dot_tn(recv_pick, inbound.reshape(peers * capacity, share)).astype(BF16)
    moved = lax.all_gather(moved, "head", axis=1, tiled=True)

    kv_weight = key_value_weight.reshape(width, 2 * HEAD_SIZE)
    queries = dot_nn(moved, w_query).astype(BF16)
    keyval = dot_nn(moved, kv_weight).astype(BF16)
    all_kv = lax.all_gather(keyval, "det", axis=0, tiled=True)
    all_kv = all_kv.reshape(-1, BLOCK_ROWS, 2 * HEAD_SIZE)
    attended, query_grad, listing = attention(
        flat_list, owners, queries, attention_cotangent, all_kv
    )
    collected = lax.all_to_all(listing, "det", split_axis=0, concat_axis=0, tiled=True)
    belongs = (wanted[None, :] == jnp.arange(blocks, dtype=jnp.int32)[:, None]).astype(BF16)
    kv_grad = dot_nn(belongs, collected.reshape(slots, -1))
    kv_grad = kv_grad.astype(BF16).reshape(row_count, 2 * HEAD_SIZE)

    partial_back = dot_nt(query_grad, w_query) + dot_nt(kv_grad, kv_weight)
    back = lax.psum_scatter(partial_back, "head", scatter_dimension=1, tiled=True).astype(BF16)
    outbound = dot_nn(recv_pick, back).astype(BF16).reshape(peers, capacity, share)
    inbound = lax.all_to_all(outbound, "det", split_axis=0, concat_axis=0, tiled=True)
    own_up = dot_tn(send_pick, inbound.reshape(peers * capacity, share)).astype(BF16)
    upstream = lax.all_gather(own_up, "head", axis=1, tiled=True)

    input_part = 0.0
    for t in range(types):
        hidden_grad = dot_nt(upstream, w_second[t]) * mask[:, t : t + 1]
        preact_grad = jax.vjp(jax.nn.gelu, preact[t])[1](hidden_grad)[0].astype(BF16)
        input_part = input_part + dot_nt(preact_grad, w_first[t])
    input_share = lax.psum_scatter(input_part, "head", scatter_dimension=1, tiled=True)
    x_grad = (own_up.astype(F32) + input_share).astype(BF16)
    return attended, x_grad


def solution(mesh):
    return jax.shard_map(
        shards,
        mesh=mesh,
        in_specs=(
            P("det", None),
            P("det"),
            P(),
            P("det", None),
            P(None, None, "head"),
            P(None, "head", None),
            P(None, "head"),
            P(None, None, "head"),
            P("det", "head"),
        ),
        out_specs=(P("det", "head"), P("det", "head")),
        check_vma=False,
    )
```

time: 614 us -> 459 us (0.75); the launches traced: 603 us -> 458 us
  other arithmetic: 121 us -> 2.36 us
  local copies, waits for them, and re-layouts: 103 us -> 6.5 us
  blocking collectives: 42.7 us -> 110 us
  Pallas kernels: 0 us -> 32.8 us
  starting transfers between devices: 35.6 us -> 16.7 us
  matrix products: 40.3 us -> 31.6 us
    all_to_all x3 -> x1, waiting for transfers between devices: 100 us -> 0.01 us  [shards(): lax.all_to_all(listing, 'det', split_axis=0, concat_axis=0, tiled=True)]
    all_gather x0 -> x1, blocking collectives: none -> 81.7 us  [shards(): all_lists = lax.all_gather(flat_list, 'det', axis=0, tiled=False)]
    gather x13 -> x0, other arithmetic: 80.3 us -> none  [the longest x6 80.3 us: unpack_rows(): slot_ids = within - starts[peer_ids]]
    all_gather x1 -> x3, waiting for transfers between devices: 55.5 us -> 129 us  [the longest x1 85.2 us: shards(): all_kv = lax.all_gather(keyval, 'det', axis=0, tiled=True)]
    psum x1 -> x0, waiting for transfers between devices: 66.3 us -> none  [shards(): mlp_sum = lax.psum(partial_mlp, 'head')]
    reduce_scatter x0 -> x2, waiting for transfers between devices: none -> 63.5 us  [the longest x1 35.1 us: shards(): mlp = lax.psum_scatter(partial, 'head', scatter_dimension=1, tiled=True)]
    gather x17 -> x0, local copies, waits for them, and re-layouts: 48.4 us -> none  [the longest x2 10.8 us: pack_rows(): source_rows[row_index.reshape(-1)]]
    psum x1 -> x0, blocking collectives: 42.7 us -> none  [shards(): back_sum = lax.psum(partial_back, 'head').astype(jnp.bfloat16)]
  transfers between devices with their start and end apart: 7 -> 8, of which waited for: 5 -> 7; matrix products, arithmetic and copies ran while one was open for 30% -> 1% of each run, Pallas kernels for 0% -> 0%
where the time goes in v1:
time: 459 us; the launch traced here: 458 us
  waiting for transfers between devices  244 us (53%)
  blocking collectives  110 us (24%)
  Pallas kernels  32.8 us (7%)
  matrix products  31.6 us (7%)
  starting transfers between devices  16.7 us (4%)
  between operations  14.3 us (3%)
  local copies, waits for them, and re-layouts  6.5 us (1%)
    all_gather x1, waiting for transfers between devices, shards(): all_kv = lax.all_gather(keyval, 'det', axis=0, tiled=True)  85.2 us
    all_gather x1, blocking collectives, shards(): all_lists = lax.all_gather(flat_list, 'det', axis=0, tiled=False)  81.7 us
    reduce_scatter x1, waiting for transfers between devices, shards(): mlp = lax.psum_scatter(partial, 'head', scatter_dimension=1, tiled=True)  35.1 us
    reduce_scatter x1, waiting for transfers between devices, shards(): lax.psum_scatter(input_part, 'head', scatter_dimension=1, tiled=True)  34.9 us
    pallas_call x1, Pallas kernels, attention(): pl.pallas_call(attention_kernel, out_shape=(jax.ShapeDtypeStruct(q.shape,...  32.8 us
    reduce_scatter x1, waiting for transfers between devices, shards(): lax.psum_scatter(partial_back, 'head', scatter_dimension=1, tiled=True)  28.3 us
    all_to_all x1, blocking collectives, shards(): lax.all_to_all(outbound, 'det', split_axis=0, concat_axis=0, tiled=True)  28 us
    all_gather x1, waiting for transfers between devices, shards(): moved = lax.all_gather(moved, 'head', axis=1, tiled=True)  21.8 us
  transfers between devices with their start and end apart: 8, of which 7 were waited for; matrix products, arithmetic and copies ran while one was open for 1% of the time, Pallas kernels for 0%

profile of v1, /device:TPU:1, one launch (start us, length us, event | category | flops | bytes accessed | tf_op | source)
XLA Modules:
  0.0 458.1 jit_solution(17743391798489543133)
XLA Ops:
  7.2 2.4 fusion.27
  10.5 1.6 copy-done.7
  13.0 2.3 convolution_add_fusion.2
  16.3 35.1 %reduce-scatter.4.cloned.1.call-done = f32[512,256]{1,0:T(8,128)} async-done(((f32[512,1024]{1,0:T(8,128)}), f32[512,256]{1,0:T(8,128)}) %reduce-scatter.4.cloned.1.call-update) | async-done | bytes 524304 | tf_op jit(solution)/shard_map/reduce_scatter | solution.py:218
  51.5 2.4 fusion.7
  53.9 10.7 %all-to-all-start = ((bf16[64,16,256]{2,1,0:T(8,128)(2,1)}), bf16[64,16,256]{2,1,0:T(8,128)(2,1)S(1)}, u32[]{:S(2)}, u32[]{:S(2)}) async-start(bf16[64,16,256]{2,1,0:T(8,128)(2,1)} %bitcast.7), calls=%async_computation.1 | async-start | bytes 1048576 | tf_op jit(solution)/shard_map/all_to_all | solution.py:223
  65.2 16.7 %all-to-all-done = bf16[64,16,256]{2,1,0:T(8,128)(2,1)S(1)} async-done(((bf16[64,16,256]{2,1,0:T(8,128)(2,1)}), bf16[64,16,256]{2,1,0:T(8,128)(2,1)S(1)}, u32[]{:S(2)}, u32[]{:S(2)}) %all-to-all-start) | async-done | bytes 524320 | tf_op jit(solution)/shard_map/all_to_all | solution.py:223
  83.6 21.8 %all-gather.5.cloned.1.call-done = bf16[512,1024]{1,0:T(8,128)(2,1)} async-done(((bf16[512,256]{1,0:T(8,128)(2,1)}), bf16[512,1024]{1,0:T(8,128)(2,1)}) %all-gather.5.cloned.1.call-update) | async-done | bytes 1048592 | tf_op jit(solution)/shard_map/all_gather | solution.py:225
  105.4 2.3 convolution_convert_fusion.2
  107.9 1.7 convolution_convert_fusion.1.q_ref
  109.6 85.2 %all-gather.7.cloned.1.call-done = bf16[32768,128]{1,0:T(8,128)(2,1)} async-done(((bf16[512,128]{1,0:T(8,128)(2,1)}), bf16[32768,128]{1,0:T(8,128)(2,1)}) %all-gather.7.cloned.1.call-update) | async-done | bytes 8388624 | tf_op jit(solution)/shard_map/all_gather | solution.py:230
  194.7 3.4 copy-done.1
  198.1 32.8 %attention.1 = (bf16[512,256]{1,0:T(8,128)(2,1)}, bf16[512,256]{1,0:T(8,128)(2,1)S(1)}, bf16[64,128,128]{2,1,0:T(8,128)(2,1)}) custom-call(s32[64]{0:T(128)S(1)} %reshape.101.list_ref, s32[64]{0:T(128)S(1)} %and_select_fusion.owner_ref, bf16[512,256]{1,0:T(8,128)(2,1)S(1)} %convolution_convert_fusion.1.q_ref, bf16[512,256]{1,0:T(8,128)(2,1)S(1)} %copy-done.2, ...), custom_call_target="tpu_custom_call" | custom-call | tf_op jit(solution)/shard_map/attention/pallas_call | solution.py:136
  230.9 5.8 %all-to-all-start.1 = ((bf16[64,128,128]{2,1,0:T(8,128)(2,1)}), bf16[64,128,128]{2,1,0:T(8,128)(2,1)S(1)}, u32[]{:S(2)}, u32[]{:S(2)}) async-start(bf16[64,128,128]{2,1,0:T(8,128)(2,1)} %get-tuple-element.7), calls=%async_computation.2 | async-start | bytes 4194304 | tf_op jit(solution)/shard_map/all_to_all | solution.py:235
  236.8 81.7 %all-gather = s32[64,1,64]{2,1,0:T(1,128)S(1)} all-gather(s32[1,1,64]{2,1,0:T(1,128)S(1)} %reshape.110), channel_id=1, replica_groups=mesh['det'=64,'head'=4] {'det'}, dimensions={0}, use_global_device_ids=true | all-gather | bytes 16640 | tf_op jit(solution)/shard_map/all_gather | solution.py:204
  320.5 1.9 convolution_add_fusion.1
  322.4 28.3 %reduce-scatter.6.cloned.1.call-done = f32[512,256]{1,0:T(8,128)} async-done(((f32[512,1024]{1,0:T(8,128)}), f32[512,256]{1,0:T(8,128)}) %reduce-scatter.6.cloned.1.call-update) | async-done | bytes 524304 | tf_op jit(solution)/shard_map/reduce_scatter | solution.py:241
  352.3 28.0 %all_to_all.15 = bf16[64,16,256]{2,1,0:T(8,128)(2,1)S(1)} all-to-all(bf16[64,16,256]{2,1,0:T(8,128)(2,1)S(1)} %bitcast.62), channel_id=1, replica_groups=mesh['det'=64,'head'=4] {'det'}, dimensions={0} | all-to-all | bytes 1048576 | tf_op jit(solution)/shard_map/all_to_all | solution.py:243
  380.3 1.6 fusion.9
  382.0 21.8 %all-gather.9.cloned.1.call-done = bf16[512,1024]{1,0:T(8,128)(2,1)} async-done(((bf16[512,256]{1,0:T(8,128)(2,1)}), bf16[512,1024]{1,0:T(8,128)(2,1)}) %all-gather.9.cloned.1.call-update) | async-done | bytes 1048592 | tf_op jit(solution)/shard_map/all_gather | solution.py:245
  403.8 5.4 %fusion.32 = f32[512,1024]{1,0:T(8,128)} fusion(f32[512,512]{1,0:T(8,128)} %copy-done.14, bf16[512,1024]{1,0:T(8,128)(2,1)} %all-gather.9.cloned.1.call-done, bf16[2,512,1024]{2,1,0:T(8,128)(2,1)} %param.14, bf16[2,1024,512]{2,1,0:T(8,128)(2,1)} %param.13, f32[512]{0:T(512)S(1)} %bitcast.68), kind=kOutput, calls=%fused_computation.46 | convolution fusion | flops 1079246848 | bytes 6293504 | tf_op jit(solution)/shard_map/dot_general | solution.py:25
  409.2 5.3 %convolution_add_fusion = f32[512,1024]{1,0:T(8,128)} fusion(f32[512,1024]{1,0:T(8,128)} %fusion.32, f32[512,512]{1,0:T(8,128)S(1)} %copy-done.6, bf16[512,1024]{1,0:T(8,128)(2,1)S(1)} %copy-done.13, bf16[2,512,1024]{2,1,0:T(8,128)(2,1)} %param.14, bf16[2,1024,512]{2,1,0:T(8,128)(2,1)} %param.13, f32[512]{0:T(512)S(1)} %bitcast.66), kind=kOutput, calls=%fused_computation.9 | convolution fusion | flops 1079771136 | bytes 8390656 | tf_op jit(solution)/shard_map/dot_general | solution.py:25
  414.5 34.9 %reduce-scatter.8.cloned.1.call-done = f32[512,256]{1,0:T(8,128)} async-done(((f32[512,1024]{1,0:T(8,128)}), f32[512,256]{1,0:T(8,128)}) %reduce-scatter.8.cloned.1.call-update) | async-done | bytes 524304 | tf_op jit(solution)/shard_map/reduce_scatter | solution.py:252
  449.4 1.8 add_convert_fusion
  (62 shorter events, 8.8 us)
Async XLA Ops:
  7.2 100.7 %copy-start = (bf16[1024,256]{1,0:T(8,128)(2,1)S(1)}, bf16[1024,256]{1,0:T(8,128)(2,1)}, u32[]{:S(2)}) copy-start(bf16[1024,256]{1,0:T(8,128)(2,1)} %param.15) | copy-start | bytes 1572868
  7.2 2.5 copy-start.11
  7.2 44.3 %reduce-scatter.4.cloned.1.call-start = ((), (), s32[]{:S(2)}) async-start(), calls=%async_computation.6 | async-start | bytes 2621440 | tf_op jit(solution)/shard_map/reduce_scatter | solution.py:218
  7.2 2.5 copy-start.12
  9.7 3.3 copy-start.5
  9.7 0.7 copy-start.10
  9.7 2.4 copy-start.7
  10.5 2.6 copy-start.14
  15.3 0.8 copy-start.8
  16.3 89.1 %copy-start.3 = (bf16[1024,2,64]{0,2,1:T(8,128)(2,1)S(1)}, bf16[1024,2,64]{0,2,1:T(8,128)(2,1)}, u32[]{:S(2)}) copy-start(bf16[1024,2,64]{0,2,1:T(8,128)(2,1)} %param.16) | copy-start | bytes 786436
  53.9 28.0 %all-to-all-start = ((bf16[64,16,256]{2,1,0:T(8,128)(2,1)}), bf16[64,16,256]{2,1,0:T(8,128)(2,1)S(1)}, u32[]{:S(2)}, u32[]{:S(2)}) async-start(bf16[64,16,256]{2,1,0:T(8,128)(2,1)} %bitcast.7), calls=%async_computation.1 | async-start | bytes 1048576 | tf_op jit(solution)/shard_map/all_to_all | solution.py:223
  64.6 43.1 %copy-start.9 = (s32[4,16]{1,0:T(4,128)S(1)}, s32[4,16]{1,0:T(4,128)}, u32[]{:S(2)}) copy-start(s32[4,16]{1,0:T(4,128)} %param.12) | copy-start | bytes 772
  64.7 40.8 %all-gather.5.cloned.1.call-start = ((), (), s32[]{:S(2)}) async-start(), calls=%async_computation.7 | async-start | bytes 1310720 | tf_op jit(solution)/shard_map/all_gather | solution.py:225
  83.5 111.2 %copy-start.2 = (bf16[512,256]{1,0:T(8,128)(2,1)S(1)}, bf16[512,256]{1,0:T(8,128)(2,1)}, u32[]{:S(2)}) copy-start(bf16[512,256]{1,0:T(8,128)(2,1)} %do_ref.1) | copy-start | bytes 786436
  83.5 111.2 %all-gather.7.cloned.1.call-start = ((), (), s32[]{:S(2)}) async-start(), calls=%async_computation.8 | async-start | bytes 8519680 | tf_op jit(solution)/shard_map/all_gather | solution.py:230
  194.7 3.4 copy-start.1
  230.9 87.7 %all-to-all-start.1 = ((bf16[64,128,128]{2,1,0:T(8,128)(2,1)}), bf16[64,128,128]{2,1,0:T(8,128)(2,1)S(1)}, u32[]{:S(2)}, u32[]{:S(2)}) async-start(bf16[64,128,128]{2,1,0:T(8,128)(2,1)} %get-tuple-element.7), calls=%async_computation.2 | async-start | bytes 4194304 | tf_op jit(solution)/shard_map/all_to_all | solution.py:235
  236.7 114.1 %reduce-scatter.6.cloned.1.call-start = ((), (), s32[]{:S(2)}) async-start(), calls=%async_computation.9 | async-start | bytes 2621440 | tf_op jit(solution)/shard_map/reduce_scatter | solution.py:241
  322.4 81.4 %all-gather.9.cloned.1.call-start = ((), (), s32[]{:S(2)}) async-start(), calls=%async_computation.10 | async-start | bytes 1310720 | tf_op jit(solution)/shard_map/all_gather | solution.py:245
  381.9 27.3 %copy-start.6 = (f32[512,512]{1,0:T(8,128)S(1)}, f32[512,512]{1,0:T(8,128)}, u32[]{:S(2)}) copy-start(f32[512,512]{1,0:T(8,128)} %copy-done.5) | copy-start | bytes 3145732
  381.9 67.5 %reduce-scatter.8.cloned.1.call-start = ((), (), s32[]{:S(2)}) async-start(), calls=%async_computation.11 | async-start | bytes 2621440 | tf_op jit(solution)/shard_map/reduce_scatter | solution.py:252
  403.8 5.4 %copy-start.13 = (bf16[512,1024]{1,0:T(8,128)(2,1)S(1)}, bf16[512,1024]{1,0:T(8,128)(2,1)}, u32[]{:S(2)}) copy-start(bf16[512,1024]{1,0:T(8,128)(2,1)} %all-gather.9.cloned.1.call-done) | copy-start | bytes 3145732
  414.5 34.9 %copy-start.4 = (bf16[512,256]{1,0:T(8,128)(2,1)S(1)}, bf16[512,256]{1,0:T(8,128)(2,1)}, u32[]{:S(2)}) copy-start(bf16[512,256]{1,0:T(8,128)(2,1)} %fusion.9) | copy-start | bytes 786436
Sparse Core Ops, SparseCore 0:
  15.4 36.0 reduce-scatter.3
  83.7 21.7 all-gather.4
  108.8 85.8 all-gather.6
  322.5 28.2 reduce-scatter.5
  382.0 21.7 all-gather.8
  414.6 34.7 reduce-scatter.7

commit v2 on v1

--- a/solution.py
+++ b/solution.py
@@ -30,7 +30,7 @@
 
 
 def attention_kernel(
-    list_ref, owner_ref, q_ref, do_ref, kv_hbm, att_ref, dq_ref, grad_ref, kv_buf, score, sems
+    list_ref, place_ref, q_ref, do_ref, kv_hbm, att_ref, dq_ref, grad_ref, kv_buf, score, sems
 ):
     blocks = q_ref.shape[0] // BLOCK_ROWS
     rows = GROUP_HEADS * BLOCK_ROWS
@@ -116,7 +116,7 @@
             grads = dot_nn(jnp.concatenate([ds, prob.astype(BF16)], axis=1), both)
             grads = grads.astype(BF16)
             for k in range(pair):
-                grad_ref[owner_ref[first + i * pair + k]] = grads[
+                grad_ref[place_ref[first + i * pair + k]] = grads[
                     k * BLOCK_ROWS : (k + 1) * BLOCK_ROWS
                 ]
             return acc
@@ -129,7 +129,7 @@
     lax.fori_loop(0, blocks, one_block, 0)
 
 
-def attention(lists, owners, q, do, kv):
+def attention(lists, places, q, do, kv):
     slots = lists.shape[0]
     vm = pl.BlockSpec(memory_space=pltpu.VMEM)
     sm = pl.BlockSpec(memory_space=pltpu.SMEM)
@@ -149,7 +149,417 @@
         ],
         compiler_params=pltpu.CompilerParams(vmem_limit_bytes=40 << 20),
         name="attention",
-    )(lists, owners, q, do, kv)
+    )(lists, places, q, do, kv)
+
+
+XS, ZS, CS, YS = 4, 8, 2, 4
+PEERS = XS * ZS * CS
+MESH = pl.DeviceIdType.MESH
+Z_ORDER = (4, 3, 5, 2, 6, 1, 7, 0)
+Y_ORDER = (2, 1, 3)
+
+
+def push(src, dst, send_sem, recv_sem, device):
+    pltpu.make_async_remote_copy(
+        src_ref=src,
+        dst_ref=dst,
+        send_sem=send_sem,
+        recv_sem=recv_sem,
+        device_id=device,
+        device_id_type=MESH,
+    ).start()
+
+
+def wait(ref, sem):
+    pltpu.make_async_copy(ref, ref, sem).wait()
+
+
+def place():
+    me = lax.axis_index("det")
+    return me, me // (ZS * CS), lax.rem(me // CS, ZS), lax.rem(me, CS), lax.axis_index("head")
+
+
+def greet():
+    me, _, _, _, y = place()
+    sem = pltpu.get_barrier_semaphore()
+
+    def signal(k, carry):
+        peer = lax.rem(me + k, PEERS)
+        pl.semaphore_signal(sem, inc=1, device_id={"det": peer}, device_id_type=MESH)
+        return carry
+
+    lax.fori_loop(1, PEERS, signal, 0)
+    for k in range(1, YS):
+        pl.semaphore_signal(sem, inc=1, device_id={"head": lax.rem(y + k, YS)}, device_id_type=MESH)
+
+
+def greeted():
+    pl.semaphore_wait(pltpu.get_barrier_semaphore(), PEERS - 1 + YS - 1)
+
+
+def span(index, size):
+    return pl.ds(pl.multiple_of(index * size, size), size)
+
+
+def scatter_sum(part, sent, landed, send_sem, recv_sem):
+    y = lax.axis_index("head")
+    for i, j in enumerate(Y_ORDER):
+        to = lax.rem(y + j, YS)
+        sent[i] = part(to).astype(BF16)
+        push(sent.at[i], landed.at[i], send_sem.at[i], recv_sem.at[i], {"head": to})
+    total = part(y)
+    for i in range(YS - 1):
+        wait(landed.at[i], recv_sem.at[i])
+        total = total + landed[i].astype(F32)
+        wait(sent.at[i], send_sem.at[i])
+    return total
+
+
+def gather_head(ref, send_sem, recv_sem):
+    y = lax.axis_index("head")
+    for i, j in enumerate(Y_ORDER):
+        to = lax.rem(y + j, YS)
+        push(ref.at[y], ref.at[y], send_sem.at[i], recv_sem.at[i], {"head": to})
+
+
+def gather_head_wait(ref, i, send_sem, recv_sem):
+    y = lax.axis_index("head")
+    source = lax.rem(y + YS - Y_ORDER[i], YS)
+    wait(ref.at[source], recv_sem.at[i])
+    wait(ref.at[source], send_sem.at[i])
+    return source
+
+
+def exchange(outbound, inbound, send_sem, recv_sem):
+    me = lax.axis_index("det")
+
+    def send(k, carry):
+        peer = lax.rem(me + k, PEERS)
+        push(outbound.at[peer], inbound.at[me], send_sem, recv_sem, {"det": peer})
+        return carry
+
+    lax.fori_loop(1, PEERS, send, 0)
+    inbound[me] = outbound[me]
+    wait(inbound.at[pl.ds(0, PEERS - 1)], recv_sem)
+    wait(outbound.at[pl.ds(0, PEERS - 1)], send_sem)
+
+
+def gather_blocks(kv, send_sem, recv_sem):
+    me, x, z, c, _ = place()
+
+    def at(jx, jz, core):
+        return (lax.rem(x + jx, XS) * ZS + lax.rem(z + jz + ZS, ZS)) * CS + core
+
+    def give(b, to):
+        push(kv.at[b], kv.at[b], send_sem, recv_sem.at[b], {"det": to})
+
+    def got(b):
+        wait(kv.at[b], recv_sem.at[b])
+
+    sister, right, left = at(0, 0, 1 - c), at(0, 1, c), at(0, -1, c)
+    others = (1, 3, 2)
+
+    @pl.when(c == 0)
+    def _():
+        for j in others:
+            give(me, at(j, 0, c))
+        for j in (0,) + others:
+            b = at(j, 0, c)
+            if j:
+                got(b)
+            give(b, right)
+            give(b, left)
+            give(b, sister)
+        for s in range(1, 5):
+            for i, j in enumerate((0,) + others):
+                reach = 4 if i % 2 == 0 else 3
+                for sign, last, to in ((-1, reach, right), (1, 7 - reach, left)):
+                    if s <= last:
+                        b = at(j, sign * s, c)
+                        got(b)
+                        if s < last:
+                            give(b, to)
+                        give(b, sister)
+
+    @pl.when(c == 1)
+    def _():
+        give(me, right)
+        give(me, left)
+        order = [0]
+        for j in others:
+            give(me, at(j, 0, c))
+        give(me, sister)
+        for s in range(1, 5):
+            for sign, last, to in ((-1, 4, right), (1, 3, left)):
+                if s <= last:
+                    order.append(sign * s)
+                    b = at(0, sign * s, c)
+                    got(b)
+                    if s < last:
+                        give(b, to)
+                    for j in others:
+                        give(b, at(j, 0, c))
+                    give(b, sister)
+        for s in order:
+            for j in others:
+                b = at(j, s, c)
+                got(b)
+                give(b, sister)
+
+    def rest(i, carry):
+        got(i * CS + 1 - c)
+        return carry
+
+    lax.fori_loop(0, PEERS // CS, rest, 0)
+    wait(kv.at[pl.ds(0, PEERS - 1)], send_sem)
+
+
+def pick_rows(column, width):
+    ids = lax.broadcasted_iota(jnp.int32, (column.shape[0], width), 1)
+    return jnp.where(column == ids, 1.0, 0.0).astype(BF16)
+
+
+def pick_slots(row, height):
+    ids = lax.broadcasted_iota(jnp.int32, (height, row.shape[1]), 0)
+    return jnp.where(row == ids, 1.0, 0.0).astype(BF16)
+
+
+def forward_kernel(
+    x_ref, mask_ref, w1_ref, w2_ref, wq_ref, wkv_ref, send_ref, recv_ref,
+    q_ref, kv_ref,
+    hidden, sent, landed, outbound, inbound, moved,
+    y_send, y_recv, g_send, g_recv, x_send, x_recv, kv_send, kv_recv,
+):
+    me, _, _, _, y = place()
+    rows, width = x_ref.shape
+    share = width // YS
+    types, _, units = w1_ref.shape
+    greet()
+    step = 256
+    for t in range(types):
+        for k in range(units // step):
+            pre = dot_nn(x_ref[...], w1_ref[t, :, k * step : (k + 1) * step])
+            act = jax.nn.gelu(pre) * mask_ref[:, t : t + 1]
+            hidden[:, t * units + k * step : t * units + (k + 1) * step] = act.astype(BF16)
+    greeted()
+    total = scatter_sum(
+        lambda g: dot_nn(hidden[...], w2_ref[:, span(g, share)]), sent, landed, y_send, y_recv
+    )
+    mixed = (x_ref[:, span(y, share)].astype(F32) + total).astype(BF16)
+    packed = dot_nn(pick_rows(send_ref[...], rows), mixed).astype(BF16)
+    outbound[...] = packed.reshape(outbound.shape)
+    exchange(outbound, inbound, x_send, x_recv)
+    slots = inbound[...].reshape(-1, share)
+    moved[y] = dot_nn(pick_slots(recv_ref[...], rows), slots).astype(BF16)
+    gather_head(moved, g_send, g_recv)
+
+    def project(g):
+        m = moved[g]
+        return dot_nn(m, wq_ref[span(g, share), :]), dot_nn(m, wkv_ref[span(g, share), :])
+
+    q, kv = project(y)
+    for i in range(YS - 1):
+        more = project(gather_head_wait(moved, i, g_send, g_recv))
+        q, kv = q + more[0], kv + more[1]
+    kv_ref[me] = kv.astype(BF16)
+    q_ref[...] = q.astype(BF16)
+    gather_blocks(kv_ref, kv_send, kv_recv)
+
+
+VM = pl.BlockSpec(memory_space=pltpu.VMEM)
+SM = pl.BlockSpec(memory_space=pltpu.SMEM)
+DMA = pltpu.SemaphoreType.DMA
+
+
+def forward(x, mask, w1, w2, wq, wkv, send_col, recv_row):
+    rows, width = x.shape
+    share = width // YS
+    capacity = 2 * rows // PEERS
+    return pl.pallas_call(
+        forward_kernel,
+        out_shape=(
+            jax.ShapeDtypeStruct((rows, wq.shape[1]), BF16),
+            jax.ShapeDtypeStruct((PEERS, rows, wkv.shape[1]), BF16),
+        ),
+        in_specs=[VM] * 8,
+        out_specs=(VM, VM),
+        scratch_shapes=[
+            pltpu.VMEM((rows, w2.shape[0]), BF16),
+            pltpu.VMEM((YS - 1, rows, share), BF16),
+            pltpu.VMEM((YS - 1, rows, share), BF16),
+            pltpu.VMEM((PEERS, capacity, share), BF16),
+            pltpu.VMEM((PEERS, capacity, share), BF16),
+            pltpu.VMEM((YS, rows, share), BF16),
+            DMA((YS - 1,)),
+            DMA((YS - 1,)),
+            DMA((YS - 1,)),
+            DMA((YS - 1,)),
+            DMA,
+            DMA,
+            DMA,
+            DMA((PEERS,)),
+        ],
+        compiler_params=pltpu.CompilerParams(
+            collective_id=1, has_side_effects=True, vmem_limit_bytes=56 << 20
+        ),
+        name="forward",
+    )(x, mask, w1, w2, wq, wkv, send_col, recv_row)
+
+
+def return_listings(
+    id_ref, g_ref, id_near, near, far_out, far_in,
+    id_send, id_recv, near_send, near_recv, far_send, far_recv,
+):
+    _, x, z, c, _ = place()
+    here = x * CS + c
+    group = XS * CS
+
+    def near_peer(j):
+        p = lax.rem(here + j, group)
+        return p, {"det": (p // CS * ZS + z) * CS + lax.rem(p, CS)}
+
+    for j in range(1, group):
+        p, to = near_peer(j)
+        push(id_ref.at[p], id_near.at[j - 1], id_send, id_recv, to)
+    for i, kz in enumerate(Z_ORDER):
+        row = lax.rem(z + kz, ZS)
+        for j in range(1, group):
+            p, to = near_peer(j)
+            push(
+                g_ref.at[p * ZS + row], near.at[i, j - 1], near_send, near_recv.at[i], to
+            )
+    blocks = far_out.shape[1]
+    total = None
+    wait(id_near, id_recv)
+    for i, kz in enumerate(Z_ORDER):
+        row = lax.rem(z + kz, ZS)
+        wait(near.at[i], near_recv.at[i])
+        sums = [0.0] * blocks
+        for j in range(group):
+            value = (near[i, j - 1] if j else g_ref[here * ZS + row]).astype(F32)
+            which = id_near[j - 1, pl.ds(row, 1), :] if j else id_ref[here, pl.ds(row, 1), :]
+            for k in range(blocks):
+                sums[k] = sums[k] + value * jnp.where(which == k, 1.0, 0.0)
+        if kz:
+            for k in range(blocks):
+                far_out[i, k] = sums[k].astype(BF16)
+            to = (x * ZS + row) * CS + c
+            push(far_out.at[i], far_in.at[i], far_send, far_recv.at[i], {"det": to})
+        else:
+            total = sums
+    for i in range(ZS - 1):
+        wait(far_in.at[i], far_recv.at[i])
+        for k in range(blocks):
+            total[k] = total[k] + far_in[i, k].astype(F32)
+    wait(id_ref.at[pl.ds(0, group - 1)], id_send)
+    wait(g_ref.at[pl.ds(0, (group - 1) * ZS)], near_send)
+    wait(far_out, far_send)
+    return total
+
+
+def backward_kernel(
+    id_ref, g_ref, dq_ref, x_ref, mask_ref, w1_ref, w2_ref, wq_ref, wkv_ref, send_ref, recv_ref,
+    out_ref,
+    id_near, near, far_out, far_in, kv_grad, slope, pre_grad, sent, landed, outbound, inbound, upstream,
+    id_send, id_recv, near_send, near_recv, far_send, far_recv,
+    y_send, y_recv, g_send, g_recv, i_send, i_recv, x_send, x_recv,
+):
+    _, _, _, _, y = place()
+    rows, width = x_ref.shape
+    share = width // YS
+    types, _, units = w1_ref.shape
+    greet()
+    step = 256
+    for t in range(types):
+        for k in range(units // step):
+            pre = dot_nn(x_ref[...], w1_ref[t, :, k * step : (k + 1) * step])
+            ones = jnp.ones_like(pre)
+            grad = jax.vjp(jax.nn.gelu, pre)[1](ones)[0] * mask_ref[:, t : t + 1]
+            slope[:, t * units + k * step : t * units + (k + 1) * step] = grad
+    greeted()
+    total = return_listings(
+        id_ref, g_ref, id_near, near, far_out, far_in,
+        id_send, id_recv, near_send, near_recv, far_send, far_recv,
+    )
+    for k in range(len(total)):
+        kv_grad[k * BLOCK_ROWS : (k + 1) * BLOCK_ROWS, :] = total[k].astype(BF16)
+
+    def back(g):
+        cols = span(g, share)
+        return dot_nt(dq_ref[...], wq_ref[cols, :]) + dot_nt(kv_grad[...], wkv_ref[cols, :])
+
+    total = scatter_sum(back, sent, landed, y_send, y_recv).astype(BF16)
+    packed = dot_nn(pick_rows(recv_ref[...], rows), total).astype(BF16)
+    outbound[...] = packed.reshape(outbound.shape)
+    exchange(outbound, inbound, x_send, x_recv)
+    slots = inbound[...].reshape(-1, share)
+    upstream[y] = dot_nn(pick_slots(send_ref[...], rows), slots).astype(BF16)
+    gather_head(upstream, g_send, g_recv)
+    for i in range(YS - 1):
+        gather_head_wait(upstream, i, g_send, g_recv)
+    for k in range(types * units // step):
+        cols = slice(k * step, (k + 1) * step)
+        grad = 0.0
+        for g in range(YS):
+            grad = grad + dot_nt(upstream[g], w2_ref[cols, g * share : (g + 1) * share])
+        pre_grad[:, cols] = (grad * slope[:, cols]).astype(BF16)
+
+    def inputs(g):
+        part = 0.0
+        for t in range(types):
+            part = part + dot_nt(
+                pre_grad[:, t * units : (t + 1) * units], w1_ref[t, span(g, share), :]
+            )
+        return part
+
+    total = scatter_sum(inputs, sent, landed, i_send, i_recv)
+    out_ref[...] = (upstream[y].astype(F32) + total).astype(BF16)
+
+
+def backward(ids, g, dq, x, mask, w1, w2, wq, wkv, send_row, recv_col):
+    rows, width = x.shape
+    share = width // YS
+    capacity = 2 * rows // PEERS
+    blocks = rows // BLOCK_ROWS
+    tile = (BLOCK_ROWS, 2 * HEAD_SIZE)
+    return pl.pallas_call(
+        backward_kernel,
+        out_shape=jax.ShapeDtypeStruct((rows, share), BF16),
+        in_specs=[VM] * 11,
+        out_specs=VM,
+        scratch_shapes=[
+            pltpu.VMEM((XS * CS - 1, ZS, 128), jnp.int32),
+            pltpu.VMEM((ZS, XS * CS - 1) + tile, BF16),
+            pltpu.VMEM((ZS - 1, blocks) + tile, BF16),
+            pltpu.VMEM((ZS - 1, blocks) + tile, BF16),
+            pltpu.VMEM((rows, 2 * HEAD_SIZE), BF16),
+            pltpu.VMEM((rows, w2.shape[0]), F32),
+            pltpu.VMEM((rows, w2.shape[0]), BF16),
+            pltpu.VMEM((YS - 1, rows, share), BF16),
+            pltpu.VMEM((YS - 1, rows, share), BF16),
+            pltpu.VMEM((PEERS, capacity, share), BF16),
+            pltpu.VMEM((PEERS, capacity, share), BF16),
+            pltpu.VMEM((YS, rows, share), BF16),
+            DMA,
+            DMA,
+            DMA,
+            DMA((ZS,)),
+            DMA,
+            DMA((ZS - 1,)),
+            DMA((YS - 1,)),
+            DMA((YS - 1,)),
+            DMA((YS - 1,)),
+            DMA((YS - 1,)),
+            DMA((YS - 1,)),
+            DMA((YS - 1,)),
+            DMA,
+            DMA,
+        ],
+        compiler_params=pltpu.CompilerParams(
+            collective_id=2, has_side_effects=True, vmem_limit_bytes=56 << 20
+        ),
+        name="backward",
+    )(ids, g, dq, x, mask, w1, w2, wq, wkv, send_row, recv_col)
 
 
 def before(counts):
@@ -162,11 +572,6 @@
     within = jnp.arange(capacity, dtype=jnp.int32)[None, :]
     rows = jnp.where(within < counts[:, None], before(counts)[:, None] + within, -1)
     return rows.reshape(-1)
-
-
-def select(slot_row, row_count):
-    ids = jnp.arange(row_count, dtype=jnp.int32)
-    return (slot_row[:, None] == ids[None, :]).astype(BF16)
 
 
 def shards(
@@ -180,77 +585,50 @@
     key_value_weight,
     attention_cotangent,
 ):
-    peers = lax.axis_size("det")
     me = lax.axis_index("det")
     row_count, width = elements.shape
-    types = w_first.shape[0]
-    share = width // lax.axis_size("head")
-    capacity = 2 * row_count // peers
-    my_columns = lax.axis_index("head") * share
-
+    types, units = w_second.shape[:2]
+    capacity = 2 * row_count // PEERS
     send_rows = slot_rows(
         lax.dynamic_index_in_dim(handover_counts, me, 0, keepdims=False), capacity
     )
     recv_rows = slot_rows(
         lax.dynamic_index_in_dim(handover_counts, me, 1, keepdims=False), capacity
     )
-    send_pick = select(send_rows, row_count)
-    recv_pick = select(recv_rows, row_count)
 
     blocks = row_count // BLOCK_ROWS
     slots = blocks * LISTED_COUNT
     flat_list = block_lists.reshape(slots)
     owners = flat_list // blocks
-    all_lists = lax.all_gather(flat_list, "det", axis=0, tiled=False)
-    held = all_lists // blocks == me
-    wanted = jnp.sum(jnp.where(held, all_lists % blocks, 0), axis=1, dtype=jnp.int32)
+    places = (owners // (ZS * CS) * CS + owners % CS) * ZS + owners // CS % ZS
+    ordered = jnp.sum(
+        jnp.where(
+            places[None, :] == jnp.arange(slots, dtype=jnp.int32)[:, None],
+            (flat_list % blocks)[None, :],
+            0,
+        ),
+        axis=1,
+        dtype=jnp.int32,
+    )
+    ids = jnp.broadcast_to(ordered.reshape(XS * CS, ZS, 1), (XS * CS, ZS, 128))
 
     mask = (element_types[:, None] == jnp.arange(types, dtype=jnp.int32)[None, :]).astype(F32)
-    preact = [jnp.dot(elements, w_first[t], preferred_element_type=F32) for t in range(types)]
-    partial = sum(
-        jnp.dot(
-            (jax.nn.gelu(preact[t]) * mask[:, t : t + 1]).astype(BF16),
-            w_second[t],
-            preferred_element_type=F32,
-        )
-        for t in range(types)
-    )
-    mlp = lax.psum_scatter(partial, "head", scatter_dimension=1, tiled=True)
-    own = lax.dynamic_slice_in_dim(elements, my_columns, share, 1)
-    mixed = (own.astype(F32) + mlp).astype(BF16)
-
-    outbound = dot_nn(send_pick, mixed).astype(BF16).reshape(peers, capacity, share)
-    inbound = lax.all_to_all(outbound, "det", split_axis=0, concat_axis=0, tiled=True)
-    moved = dot_tn(recv_pick, inbound.reshape(peers * capacity, share)).astype(BF16)
-    moved = lax.all_gather(moved, "head", axis=1, tiled=True)
-
+    w2 = w_second.reshape(types * units, width)
     kv_weight = key_value_weight.reshape(width, 2 * HEAD_SIZE)
-    queries = dot_nn(moved, w_query).astype(BF16)
-    keyval = dot_nn(moved, kv_weight).astype(BF16)
-    all_kv = lax.all_gather(keyval, "det", axis=0, tiled=True)
-    all_kv = all_kv.reshape(-1, BLOCK_ROWS, 2 * HEAD_SIZE)
+    queries, all_kv = forward(
+        elements, mask, w_first, w2, w_query, kv_weight, send_rows[:, None], recv_rows[None, :]
+    )
     attended, query_grad, listing = attention(
-        flat_list, owners, queries, attention_cotangent, all_kv
-    )
-    collected = lax.all_to_all(listing, "det", split_axis=0, concat_axis=0, tiled=True)
-    belongs = (wanted[None, :] == jnp.arange(blocks, dtype=jnp.int32)[:, None]).astype(BF16)
-    kv_grad = dot_nn(belongs, collected.reshape(slots, -1))
-    kv_grad = kv_grad.astype(BF16).reshape(row_count, 2 * HEAD_SIZE)
-
-    partial_back = dot_nt(query_grad, w_query) + dot_nt(kv_grad, kv_weight)
-    back = lax.psum_scatter(partial_back, "head", scatter_dimension=1, tiled=True).astype(BF16)
-    outbound = dot_nn(recv_pick, back).astype(BF16).reshape(peers, capacity, share)
-    inbound = lax.all_to_all(outbound, "det", split_axis=0, concat_axis=0, tiled=True)
-    own_up = dot_tn(send_pick, inbound.reshape(peers * capacity, share)).astype(BF16)
-    upstream = lax.all_gather(own_up, "head", axis=1, tiled=True)
-
-    input_part = 0.0
-    for t in range(types):
-        hidden_grad = dot_nt(upstream, w_second[t]) * mask[:, t : t + 1]
-        preact_grad = jax.vjp(jax.nn.gelu, preact[t])[1](hidden_grad)[0].astype(BF16)
-        input_part = input_part + dot_nt(preact_grad, w_first[t])
-    input_share = lax.psum_scatter(input_part, "head", scatter_dimension=1, tiled=True)
-    x_grad = (own_up.astype(F32) + input_share).astype(BF16)
+        flat_list,
+        places,
+        queries,
+        attention_cotangent,
+        all_kv.reshape(-1, BLOCK_ROWS, 2 * HEAD_SIZE),
+    )
+    x_grad = backward(
+        ids, listing, query_grad, elements, mask, w_first, w2, w_query, kv_weight,
+        send_rows[None, :], recv_rows[:, None],
+    )
     return attended, x_grad
 
 

time: 459 us -> 246 us (0.54)
  waiting for transfers between devices: 244 us -> 0 us
  Pallas kernels: 32.8 us -> 228 us
  blocking collectives: 110 us -> 0 us
  matrix products: 31.6 us -> 0 us
  starting transfers between devices: 16.7 us -> 0 us
  between operations: 14.3 us -> 0.73 us
  local copies, waits for them, and re-layouts: 6.5 us -> 15.2 us
    pallas_call x0 -> x2, Pallas kernels: none -> 196 us  [the longest x1 100 us: backward(): pl.pallas_call(backward_kernel, out_shape=jax.ShapeDtypeStruct((rows, sha...]
    all_gather x3 -> x0, waiting for transfers between devices: 129 us -> none  [the longest x1 85.2 us: shards(): all_kv = lax.all_gather(keyval, 'det', axis=0, tiled=True)]
    reduce_scatter x3 -> x0, waiting for transfers between devices: 98.4 us -> none  [the longest x1 35.1 us: shards(): mlp = lax.psum_scatter(partial, 'head', scatter_dimension=1, tiled=True)]
    all_gather x1 -> x0, blocking collectives: 81.7 us -> none  [shards(): all_lists = lax.all_gather(flat_list, 'det', axis=0, tiled=False)]
    dot_general x15 -> x0, matrix products: 31.6 us -> none  [the longest x4 13 us: dot_nt(): lax.dot_general(a, b, (((1,), (1,)), ((), ())), preferred_element_type=F32)]
    all_to_all x1 -> x0, blocking collectives: 28 us -> none  [shards(): lax.all_to_all(outbound, 'det', split_axis=0, concat_axis=0, tiled=True)]
    all_to_all x2 -> x0, waiting for transfers between devices: 16.8 us -> none  [the longest x1 16.7 us: shards(): lax.all_to_all(outbound, 'det', split_axis=0, concat_axis=0, tiled=True)]
    all_to_all x2 -> x0, starting transfers between devices: 16.5 us -> none  [the longest x1 10.7 us: shards(): lax.all_to_all(outbound, 'det', split_axis=0, concat_axis=0, tiled=True)]
  transfers between devices with their start and end apart: 8 -> 0, of which waited for: 7 -> 0; matrix products, arithmetic and copies ran while one was open for 1% -> 0% of each run, Pallas kernels for 0% -> 0%
where the time goes in v2:
time: 246 us
  Pallas kernels  228 us (93%)
  local copies, waits for them, and re-layouts  15.2 us (6%)
    pallas_call x1, Pallas kernels, backward(): pl.pallas_call(backward_kernel, out_shape=jax.ShapeDtypeStruct((rows, sha...  100 us
    pallas_call x1, Pallas kernels, forward(): pl.pallas_call(forward_kernel, out_shape=(jax.ShapeDtypeStruct((rows, wq....  95.4 us
    pallas_call x1, Pallas kernels, attention(): pl.pallas_call(attention_kernel, out_shape=(jax.ShapeDtypeStruct(q.shape,...  32 us
    unnamed x15, local copies, waits for them, and re-layouts  8.8 us

profile of v2, /device:TPU:1, one launch (start us, length us, event | category | flops | bytes accessed | tf_op | source)
XLA Modules:
  0.0 246.0 jit_solution(10179751602518164345)
XLA Ops:
  0.6 0.7 copy-done
  1.4 0.1 select_reduce_fusion.2
  1.5 0.1 add_select_fusion.1
  1.6 1.1 select_n.129.send_ref
  2.8 0.2 dynamic-slice_reduce_fusion
  2.9 0.1 select_reduce_fusion.1
  3.1 0.1 add_select_fusion
  3.2 0.7 select_n.124.recv_ref
  3.8 1.8 copy.16.wkv_ref
  5.6 1.5 fusion.mask_ref
  7.2 95.4 %forward.1 = (bf16[512,256]{1,0:T(8,128)(2,1)}, bf16[64,512,128]{2,1,0:T(8,128)(2,1)}) custom-call(bf16[512,1024]{1,0:T(8,128)(2,1)} %x_ref.3, f32[512,2]{1,0:T(8,128)} %fusion.mask_ref, bf16[2,1024,512]{2,1,0:T(8,128)(2,1)} %w1_ref.3, bf16[1024,1024]{1,0:T(8,128)(2,1)} %bitcast.6, bf16[1024,256]{1,0:T(8,128)(2,1)} %wq_ref.3, ...), custom_call_target="tpu_custom_call" | custom-call | tf_op jit(solution)/shard_map/forward/pallas_call | solution.py:378
  102.6 0.1 reshape.321.list_ref
  102.8 3.4 %copy-done.1 = bf16[64,512,128]{2,1,0:T(8,128)(2,1)S(1)} copy-done((bf16[64,512,128]{2,1,0:T(8,128)(2,1)S(1)}, bf16[64,512,128]{2,1,0:T(8,128)(2,1)}, u32[]{:S(2)}) %copy-start.1) | copy-done | bytes 8388632
  106.1 0.9 copy-done.5
  107.1 32.0 %attention.1 = (bf16[512,256]{1,0:T(8,128)(2,1)}, bf16[512,256]{1,0:T(8,128)(2,1)S(1)}, bf16[64,128,128]{2,1,0:T(8,128)(2,1)S(1)}) custom-call(s32[64]{0:T(128)S(1)} %reshape.321.list_ref, s32[64]{0:T(128)S(1)} %get-tuple-element.13.place_ref, bf16[512,256]{1,0:T(8,128)(2,1)S(1)} %copy-done.5, bf16[512,256]{1,0:T(8,128)(2,1)S(1)} %copy-done.3, ...), custom_call_target="tpu_custom_call" | custom-call | tf_op jit(solution)/shard_map/attention/pallas_call | solution.py:136
  139.2 1.3 copy-done.2
  140.5 0.7 copy-done.4
  141.2 1.1 select_n.130.recv_ref
  142.3 0.7 select_n.127.send_ref
  143.0 0.1 select_reduce_fusion
  143.1 0.1 broadcast_in_dim.58
  143.2 0.7 broadcast_in_dim.59.id_ref
  143.9 100.5 %backward.1 = bf16[512,256]{1,0:T(8,128)(2,1)} custom-call(s32[8,8,128]{2,1,0:T(8,128)} %broadcast_in_dim.59.id_ref, bf16[64,128,128]{2,1,0:T(8,128)(2,1)} %copy-done.2, bf16[512,256]{1,0:T(8,128)(2,1)} %copy-done.4, bf16[512,1024]{1,0:T(8,128)(2,1)} %x_ref.3, f32[512,2]{1,0:T(8,128)} %fusion.mask_ref, bf16[2,1024,512]{2,1,0:T(8,128)(2,1)} %w1_ref.3, ...), custom_call_target="tpu_custom_call" | custom-call | tf_op jit(solution)/shard_map/backward/pallas_call | solution.py:525
  244.3 1.7 copy.21
  (11 shorter events, 0.1 us)
Async XLA Ops:
  0.6 0.8 copy-start
  7.2 95.5 %copy-start.6 = (s32[4,16]{1,0:T(4,128)S(1)}, s32[4,16]{1,0:T(4,128)}, u32[]{:S(2)}) copy-start(s32[4,16]{1,0:T(4,128)} %param.12) | copy-start | bytes 772
  7.2 95.6 %copy-start.3 = (bf16[512,256]{1,0:T(8,128)(2,1)S(1)}, bf16[512,256]{1,0:T(8,128)(2,1)}, u32[]{:S(2)}) copy-start(bf16[512,256]{1,0:T(8,128)(2,1)} %do_ref.1) | copy-start | bytes 786436
  102.8 3.4 %copy-start.1 = (bf16[64,512,128]{2,1,0:T(8,128)(2,1)S(1)}, bf16[64,512,128]{2,1,0:T(8,128)(2,1)}, u32[]{:S(2)}) copy-start(bf16[64,512,128]{2,1,0:T(8,128)(2,1)} %get-tuple-element.8) | copy-start | bytes 25165828
  106.1 0.9 copy-start.5
  139.1 1.4 copy-start.2
  140.5 0.7 copy-start.4

commit v3 on v1

v3 whole, which is shorter than its diff:
```python
import functools

import jax
import jax.numpy as jnp
from jax import lax
from jax.experimental import pallas as pl
from jax.experimental.pallas import tpu as pltpu
from jax.sharding import PartitionSpec as P

HEAD_SIZE = 64
BLOCK_ROWS = 128
LISTED_COUNT = 16
GROUP_HEADS = 4
SCALE = HEAD_SIZE ** (-0.5)

F32 = jnp.float32
BF16 = jnp.bfloat16


def dot_nn(a, b):
    return lax.dot_general(a, b, (((1,), (0,)), ((), ())), preferred_element_type=F32)


def dot_nt(a, b):
    return lax.dot_general(a, b, (((1,), (1,)), ((), ())), preferred_element_type=F32)


def dot_tn(a, b):
    return lax.dot_general(a, b, (((0,), (0,)), ((), ())), preferred_element_type=F32)


XS, ZS, CS, YS = 4, 8, 2, 4
PEERS = XS * ZS * CS
MESH = pl.DeviceIdType.MESH
Z_ORDER = (4, 3, 5, 2, 6, 1, 7, 0)
Y_ORDER = (2, 1, 3)


def push(src, dst, send_sem, recv_sem, device):
    pltpu.make_async_remote_copy(
        src_ref=src,
        dst_ref=dst,
        send_sem=send_sem,
        recv_sem=recv_sem,
        device_id=device,
        device_id_type=MESH,
    ).start()


def wait(ref, sem):
    pltpu.make_async_copy(ref, ref, sem).wait()


def place():
    me = lax.axis_index("det")
    return me, me // (ZS * CS), lax.rem(me // CS, ZS), lax.rem(me, CS), lax.axis_index("head")


def greet():
    me, _, _, _, y = place()
    sem = pltpu.get_barrier_semaphore()

    def signal(k, carry):
        peer = lax.rem(me + k, PEERS)
        pl.semaphore_signal(sem, inc=1, device_id={"det": peer}, device_id_type=MESH)
        return carry

    lax.fori_loop(1, PEERS, signal, 0)
    for k in range(1, YS):
        pl.semaphore_signal(sem, inc=1, device_id={"head": lax.rem(y + k, YS)}, device_id_type=MESH)


def greeted():
    pl.semaphore_wait(pltpu.get_barrier_semaphore(), PEERS - 1 + YS - 1)


def span(index, size):
    return pl.ds(pl.multiple_of(index * size, size), size)


def upright(row):
    return jnp.broadcast_to(row.astype(F32), (8, row.shape[1])).T[:, 0:1]


def slot_rows(counts, me, capacity):
    peers = counts.shape[0]
    down = lax.broadcasted_iota(jnp.int32, counts.shape, 0)
    along = lax.broadcasted_iota(jnp.int32, counts.shape, 1)
    own = jnp.sum(jnp.where(down == me, counts, 0.0), axis=0, keepdims=True)
    start = jnp.sum(jnp.where(down < along, upright(own), 0.0), axis=0, keepdims=True)
    wide = (peers, peers * capacity)
    peer = lax.broadcasted_iota(jnp.int32, wide, 1) // capacity
    mine = jnp.where(peer == lax.broadcasted_iota(jnp.int32, wide, 0), 1.0, 0.0)

    def expand(row):
        return jnp.sum(jnp.where(mine > 0.5, upright(row), 0.0), axis=0, keepdims=True)

    within = lax.rem(lax.broadcasted_iota(jnp.int32, (1, wide[1]), 1), capacity).astype(F32)
    return jnp.where(within < expand(own), expand(start) + within, -1.0)


def pick_rows(column, width):
    ids = lax.broadcasted_iota(jnp.int32, (column.shape[0], width), 1).astype(F32)
    return jnp.where(column == ids, 1.0, 0.0).astype(BF16)


def pick_slots(row, height):
    ids = lax.broadcasted_iota(jnp.int32, (height, row.shape[1]), 0).astype(F32)
    return jnp.where(row == ids, 1.0, 0.0).astype(BF16)


HALVES = 2
WIDE = 4


def spread_start(part, sent, landed, send_sem, recv_sem):
    y = lax.axis_index("head")
    half = sent.shape[-1]
    devices = [{"head": lax.rem(y + j, YS)} for j in Y_ORDER]

    def give(h, i):
        push(sent.at[h, i], landed.at[h, i], send_sem.at[h, i], recv_sem.at[h, i], devices[i])

    for i, j in enumerate(Y_ORDER):
        value = part(lax.rem(y + j, YS)).astype(BF16)
        for h in range(HALVES):
            sent[h, i] = value[:, h * half : (h + 1) * half]
        give(0, i)
    for h in range(1, HALVES):
        for i in range(YS - 1):
            give(h, i)
    return part(y)


def spread_sum(own, h, sent, landed, send_sem, recv_sem):
    half = sent.shape[-1]
    total = own[:, h * half : (h + 1) * half]
    for i in range(YS - 1):
        wait(landed.at[h, i], recv_sem.at[h, i])
        total = total + landed[h, i].astype(F32)
        wait(sent.at[h, i], send_sem.at[h, i])
    return total


class Sum:
    def __init__(self, bufs):
        (self.far, self.far_in, self.near, self.near_in, self.hold,
         self.fs, self.fr, self.ns, self.nr) = bufs
        self.y = lax.axis_index("head")
        self.way = (lax.rem(self.y + 1, YS), lax.rem(self.y + YS - 1, YS))
        rows, self.half = self.far.shape[1:]
        self.rows = (pl.ds(0, rows // 2), pl.ds(rows // 2, rows // 2))
        self.cut = rows // 2

    def give_far(self, h, w):
        r = self.rows[w]
        push(
            self.far.at[h, r], self.far_in.at[h, r], self.fs.at[h, w], self.fr.at[h, w],
            {"head": self.way[w]},
        )

    def give_near(self, h, w, k):
        r = self.rows[k]
        push(
            self.near.at[h, w, r], self.near_in.at[h, w, r], self.ns.at[h, w, k],
            self.nr.at[h, w, k], {"head": self.way[w]},
        )

    def start(self, part):
        half = self.half
        value = part(lax.rem(self.y + 2, YS)).astype(BF16)
        for h in range(HALVES):
            self.far[h] = value[:, h * half : (h + 1) * half]
            for w in range(2):
                self.give_far(h, w)
        for w in range(2):
            value = part(self.way[w])
            mine = slice(w * self.cut, (w + 1) * self.cut)
            rest = slice((1 - w) * self.cut, (2 - w) * self.cut)
            self.hold[w] = value[mine]
            early = value[rest].astype(BF16)
            for h in range(HALVES):
                self.near[h, w, self.rows[1 - w], :] = early[:, h * half : (h + 1) * half]
                self.give_near(h, w, 1 - w)
        self.own = part(self.y)

    def relay(self, h):
        for w in range(2):
            r = self.rows[w]
            wait(self.far_in.at[h, r], self.fr.at[h, w])
            cols = slice(h * self.half, (h + 1) * self.half)
            value = self.hold[w, :, cols] + self.far_in[h, r, :].astype(F32)
            self.near[h, w, r, :] = value.astype(BF16)
            self.give_near(h, w, w)

    def finish(self, h):
        total = self.own[:, h * self.half : (h + 1) * self.half]
        for w in range(2):
            for k in (1 - w, w):
                wait(self.near_in.at[h, w, self.rows[k]], self.nr.at[h, w, k])
            total = total + self.near_in[h, w].astype(F32)
        return total

    def drain(self):
        for h in range(HALVES):
            for w in range(2):
                wait(self.far.at[h, self.rows[w]], self.fs.at[h, w])
                for k in range(2):
                    wait(self.near.at[h, w, self.rows[k]], self.ns.at[h, w, k])


def exchange_start(outbound, inbound, send_sem, recv_sem):
    me = lax.axis_index("det")

    def send(k, carry):
        peer = lax.rem(me + k, PEERS)
        push(outbound.at[peer], inbound.at[me], send_sem, recv_sem, {"det": peer})
        return carry

    lax.fori_loop(1, PEERS, send, 0)
    inbound[me] = outbound[me]


def exchange_wait(outbound, inbound, send_sem, recv_sem):
    wait(inbound.at[pl.ds(0, PEERS - 1)], recv_sem)
    wait(outbound.at[pl.ds(0, PEERS - 1)], send_sem)


def join_start(ref, send_sem, recv_sem):
    y = lax.axis_index("head")
    for i, j in enumerate(Y_ORDER):
        to = lax.rem(y + j, YS)
        push(ref.at[y], ref.at[y], send_sem.at[i], recv_sem.at[i], {"head": to})


def join_wait(ref, i, send_sem, recv_sem):
    y = lax.axis_index("head")
    source = lax.rem(y + YS - Y_ORDER[i], YS)
    wait(ref.at[source], recv_sem.at[i])
    wait(ref.at[source], send_sem.at[i])
    return source


class Handover:
    def __init__(self, bufs):
        (self.sent, self.landed, self.out, self.inb, self.full,
         self.ss, self.sr, self.es, self.er, self.js, self.jr) = bufs

    def run(self, part, finish, pack, unpack):
        rows = self.full.shape[2]
        y = lax.axis_index("head")
        own = spread_start(part, self.sent, self.landed, self.ss, self.sr)
        for h in range(HALVES):
            value = finish(spread_sum(own, h, self.sent, self.landed, self.ss, self.sr), h)
            packed = dot_nn(pack, value).astype(BF16)
            self.out[h] = packed.reshape(self.out.shape[1:])
            exchange_start(self.out.at[h], self.inb.at[h], self.es.at[h], self.er.at[h])
        for h in range(HALVES):
            exchange_wait(self.out.at[h], self.inb.at[h], self.es.at[h], self.er.at[h])
            slots = self.inb[h].reshape(-1, self.inb.shape[-1])
            self.full[h, y] = dot_nn(unpack, slots).astype(BF16)
            join_start(self.full.at[h], self.js.at[h], self.jr.at[h])

    def parts(self):
        y = lax.axis_index("head")
        for h in range(HALVES):
            yield h, y
            for i in range(YS - 1):
                yield h, join_wait(self.full.at[h], i, self.js.at[h], self.jr.at[h])


class Spread:
    def __init__(self, ref, send_sem, recv_sem):
        self.ref, self.send_sem, self.recv_sem = ref, send_sem, recv_sem
        _, self.x, self.z, self.c, _ = place()
        self.sister, self.right, self.left = (
            self.at(0, 0, 1 - self.c), self.at(0, 1, self.c), self.at(0, -1, self.c)
        )
        others = (1, 3, 2)
        self.first, second = [], []
        for j in (0,) + others:
            self.first.append((0, j, 0, (0, 1, 2) if j else (0, 1, 2, 3)))
        for s in range(1, 5):
            for i, j in enumerate((0,) + others):
                reach = 4 if i % 2 == 0 else 3
                for sign, last, way in ((-1, reach, 0), (1, 7 - reach, 1)):
                    if s <= last:
                        self.first.append((1, j, sign * s, ((way,) if s < last else ()) + (2,)))
        second.append((0, 0, 0, (0, 1, 3, 2)))
        order = [0]
        for s in range(1, 5):
            for sign, last, way in ((-1, 4, 0), (1, 3, 1)):
                if s <= last:
                    order.append(sign * s)
                    second.append((1, 0, sign * s, ((way,) if s < last else ()) + (3, 2)))
        for s in order:
            for j in others:
                second.append((1, j, s, (2,)))
        self.second = second
        self.others = others

    def at(self, jx, jz, core):
        return (lax.rem(self.x + jx, XS) * ZS + lax.rem(self.z + jz + ZS, ZS)) * CS + core

    def blocks(self, b, count=1):
        n = self.ref.shape[0] // PEERS
        return self.ref.at[pl.ds(b * n, count * n)]

    def do(self, event):
        kind, jx, jz, ways = event
        b = self.at(jx, jz, self.c)
        if kind or jx or jz:
            wait(self.blocks(b), self.recv_sem.at[b])
        for way in ways:
            if way == 3:
                targets = [self.at(j, 0, self.c) for j in self.others]
            else:
                targets = [(self.right, self.left, self.sister)[way]]
            for to in targets:
                push(
                    self.blocks(b), self.blocks(b), self.send_sem, self.recv_sem.at[b], {"det": to}
                )

    def event(self, i, when=None):
        for core, events in ((0, self.first), (1, self.second)):
            if i < len(events):
                cond = self.c == core
                if when is not None:
                    cond = jnp.logical_and(cond, when)
                pl.when(cond)(functools.partial(self.do, events[i]))

    def count(self):
        return max(len(self.first), len(self.second))

    def finish(self):
        def rest(i, carry):
            b = i * CS + 1 - self.c
            wait(self.blocks(b), self.recv_sem.at[b])
            return carry

        lax.fori_loop(0, PEERS // CS, rest, 0)
        wait(self.blocks(0, PEERS - 1), self.send_sem)


class Return:
    def __init__(self, id_ref, id_near, bufs):
        (self.g, self.near, self.far_out, self.far_in,
         self.near_send, self.near_recv, self.far_send, self.far_recv) = bufs
        self.id_ref, self.id_near = id_ref, id_near
        _, self.x, self.z, self.c, _ = place()
        self.here = self.x * CS + self.c
        self.group = XS * CS
        self.total = None

    def peer(self, j):
        p = lax.rem(self.here + j, self.group)
        return p, {"det": (p // CS * ZS + self.z) * CS + lax.rem(p, CS)}

    def start(self):
        for i, kz in enumerate(Z_ORDER):
            row = lax.rem(self.z + kz, ZS)
            for j in range(1, self.group):
                p, to = self.peer(j)
                push(
                    self.g.at[p * ZS + row], self.near.at[i, j - 1],
                    self.near_send, self.near_recv.at[i], to,
                )

    def combine(self, i):
        blocks = self.far_out.shape[1]
        row = lax.rem(self.z + Z_ORDER[i], ZS)
        wait(self.near.at[i], self.near_recv.at[i])
        sums = [0.0] * blocks
        for j in range(self.group):
            value = (self.near[i, j - 1] if j else self.g[self.here * ZS + row]).astype(F32)
            if j:
                which = self.id_near[j - 1, pl.ds(row, 1), :]
            else:
                which = self.id_ref[self.here, pl.ds(row, 1), :]
            for k in range(blocks):
                sums[k] = sums[k] + value * jnp.where(which == k, 1.0, 0.0)
        if i == ZS - 1:
            return sums
        for k in range(blocks):
            self.far_out[i, k] = sums[k].astype(BF16)
        to = (self.x * ZS + row) * CS + self.c
        push(
            self.far_out.at[i], self.far_in.at[i], self.far_send, self.far_recv.at[i], {"det": to}
        )
        return None

    def finish(self, total):
        for i in range(ZS - 1):
            wait(self.far_in.at[i], self.far_recv.at[i])
            for k in range(len(total)):
                total[k] = total[k] + self.far_in[i, k].astype(F32)
        wait(self.g.at[pl.ds(0, (self.group - 1) * ZS)], self.near_send)
        wait(self.far_out, self.far_send)
        return jnp.concatenate(total, axis=1)


def head_rows(value):
    t = value.T
    return jnp.concatenate(
        [t[g * HEAD_SIZE : (g + 1) * HEAD_SIZE] for g in range(GROUP_HEADS)], axis=1
    )


def head_columns(value):
    return jnp.concatenate(
        [value[:, g * BLOCK_ROWS : (g + 1) * BLOCK_ROWS] for g in range(GROUP_HEADS)], axis=0
    ).T


def kernel(
    list_ref, slot_ref, x_ref, kind_ref, do_ref, w1_ref, w2_ref, wq_ref, wkv_ref,
    count_ref,
    att_ref, out_ref,
    hidden, slope, pick_a, pick_b, q_t, do_t, kvt, score, prob, glist, stat, dq, kv_grad,
    id_own, id_near,
    *rest,
):
    rest = list(rest)

    def take(n):
        got = rest[:n]
        del rest[:n]
        return got

    there, back = Handover(take(11)), Handover(take(11))
    blocks_of = Spread(kvt, *take(2))
    id_send, id_recv = take(2)
    ret_v = Return(id_own, id_near, take(8))
    ret_k = Return(id_own, id_near, take(8))
    last = Sum(take(9))

    me, _, _, _, y = place()
    rows, width = x_ref.shape
    share = width // YS
    half = share // HALVES
    types, _, units = w1_ref.shape
    blocks = rows // BLOCK_ROWS
    lanes = GROUP_HEADS * BLOCK_ROWS
    greet()

    def name(p, carry):
        slot = slot_ref[p]
        which = lax.rem(list_ref[slot // LISTED_COUNT, lax.rem(slot, LISTED_COUNT)], blocks)
        id_own[p // ZS, pl.ds(lax.rem(p, ZS), 1), :] = jnp.full((1, 128), which, jnp.int32)
        return carry

    lax.fori_loop(0, XS * CS * ZS, name, 0)
    counts = count_ref[...].astype(F32)
    capacity = there.out.shape[2]
    send_row = slot_rows(counts, me, capacity)
    recv_row = slot_rows(counts.T, me, capacity)
    kinds = upright(kind_ref[...])
    step = 256
    for t in range(types):
        for k in range(units // step):
            cols = slice(t * units + k * step, t * units + (k + 1) * step)
            pre = dot_nn(x_ref[...], w1_ref[t, :, k * step : (k + 1) * step])
            keep = jnp.where(kinds == t, 1.0, 0.0)
            act, pull = jax.vjp(jax.nn.gelu, pre)
            hidden[:, cols] = (act * keep).astype(BF16)
            slope[:, cols] = pull(jnp.ones_like(pre))[0] * keep
    greeted()
    for j in range(1, XS * CS):
        p, to = ret_v.peer(j)
        push(id_own.at[p], id_near.at[j - 1], id_send, id_recv, to)
    pick_a[...] = pick_rows(upright(send_row), rows)
    pick_b[...] = pick_slots(recv_row, rows)

    def finish_there(total, h):
        own = x_ref[:, pl.ds(pl.multiple_of(y * share + h * half, half), half)]
        return (own.astype(F32) + total).astype(BF16)

    there.run(
        lambda g: dot_nn(hidden[...], w2_ref[:, span(g, share)]),
        finish_there, pick_a[...], pick_b[...],
    )
    for b in range(blocks):
        do_t[b] = head_rows(do_ref[b * BLOCK_ROWS : (b + 1) * BLOCK_ROWS, :].astype(F32)).astype(
            BF16
        )
    q, kv = 0.0, 0.0
    for h, g in there.parts():
        m = there.full[h, g]
        cols = pl.ds(pl.multiple_of(g * share + h * half, half), half)
        q = q + dot_nn(m, wq_ref[cols, :])
        kv = kv + dot_nt(wkv_ref[:, cols], m)
    kv = kv.astype(BF16)
    for b in range(blocks):
        cols = slice(b * BLOCK_ROWS, (b + 1) * BLOCK_ROWS)
        kvt[me * blocks + b] = kv[:, cols]
    for i in range(blocks_of.count()):
        blocks_of.event(i)
        if i == 0:
            q = q.astype(BF16).astype(F32) * SCALE
            for b in range(blocks):
                q_t[b] = head_rows(q[b * BLOCK_ROWS : (b + 1) * BLOCK_ROWS, :]).astype(BF16)
    blocks_of.finish()

    pieces = LISTED_COUNT // WIDE
    span_keys = WIDE * BLOCK_ROWS

    def listed(b, first, part):
        rows_of = slice(part * HEAD_SIZE, (part + 1) * HEAD_SIZE)
        return jnp.concatenate(
            [kvt[list_ref[b, first + k], rows_of, :] for k in range(WIDE)], axis=1
        )

    def soft(b, carry):
        base = b * LISTED_COUNT
        top = jnp.full((8, lanes), -jnp.inf, F32)
        for i in range(pieces):
            value = dot_tn(listed(b, i * WIDE, 0), q_t[b])
            score[i * span_keys : (i + 1) * span_keys, :] = value
            top = jnp.maximum(top, jnp.max(value.reshape(-1, 8, lanes), axis=0))
        top = jnp.max(top, axis=0, keepdims=True)
        total = jnp.zeros((8, lanes), F32)
        for i in range(pieces):
            value = jnp.exp(score[i * span_keys : (i + 1) * span_keys, :] - top)
            total = total + jnp.sum(value.reshape(-1, 8, lanes), axis=0)
            prob[b, i * span_keys : (i + 1) * span_keys, :] = value.astype(BF16)
        inverse = 1.0 / jnp.sum(total, axis=0, keepdims=True)
        stat[b] = jnp.broadcast_to(inverse, (8, lanes))
        scaled = (do_t[b].astype(F32) * inverse).astype(BF16)
        for i in range(pieces):
            grad = dot_nt(scaled, prob[b, i * span_keys : (i + 1) * span_keys, :]).astype(BF16)
            for k in range(WIDE):
                glist[base + i * WIDE + k] = grad[:, k * BLOCK_ROWS : (k + 1) * BLOCK_ROWS]
        return carry

    lax.fori_loop(0, blocks, soft, 0)

    def reorder(ref):
        def one(i, carry):
            ref[i] = glist[slot_ref[i]]
            return carry

        lax.fori_loop(0, ref.shape[0], one, 0, unroll=8)

    reorder(ret_v.g)
    ret_v.start()
    wait(id_near, id_recv)
    wait(id_own.at[pl.ds(0, XS * CS - 1)], id_send)

    def grads(b, carry):
        base = b * LISTED_COUNT
        acc = jnp.zeros((HEAD_SIZE, lanes), F32)
        for i in range(pieces):
            acc = acc + dot_nn(
                listed(b, i * WIDE, 1), prob[b, i * span_keys : (i + 1) * span_keys, :]
            )
        for k in range(1, blocks):
            pl.when(b == k)(functools.partial(ret_v.combine, k - 1))
        inverse = stat[b, 0:1, :]
        out_t = acc * inverse
        where = pl.ds(pl.multiple_of(b * BLOCK_ROWS, BLOCK_ROWS), BLOCK_ROWS)
        att_ref[where, :] = head_columns(out_t)
        d = do_t[b]
        delta = jnp.sum(out_t * d.astype(F32), axis=0, keepdims=True)
        acc = jnp.zeros((HEAD_SIZE, lanes), F32)
        for i in range(pieces):
            p = prob[b, i * span_keys : (i + 1) * span_keys, :].astype(F32) * inverse
            dp = dot_tn(listed(b, i * WIDE, 1), d)
            ds = (p * (dp - delta)).astype(BF16)
            acc = acc + dot_nn(listed(b, i * WIDE, 0), ds)
            grad = dot_nt(q_t[b], ds).astype(BF16)
            for k in range(WIDE):
                glist[base + i * WIDE + k] = grad[:, k * BLOCK_ROWS : (k + 1) * BLOCK_ROWS]
        dq[where, :] = head_columns(acc * SCALE).astype(BF16)
        return carry

    lax.fori_loop(0, blocks, grads, 0)
    reorder(ret_k.g)
    ret_k.start()
    for i in range(blocks - 1, ZS - 1):
        ret_v.combine(i)
    total = ret_v.combine(ZS - 1)
    for i in range(4):
        ret_k.combine(i)
    total = ret_v.finish(total)
    kv_grad[:, HEAD_SIZE:] = total.T.astype(BF16)
    for i in range(4, ZS - 1):
        ret_k.combine(i)
    pick_a[...] = pick_rows(upright(recv_row), rows)
    pick_b[...] = pick_slots(send_row, rows)
    total = ret_k.finish(ret_k.combine(ZS - 1))
    kv_grad[:, :HEAD_SIZE] = total.T.astype(BF16)

    def back_part(g):
        cols = span(g, share)
        return dot_nt(dq[...], wq_ref[cols, :]) + dot_nn(kv_grad[...], wkv_ref[:, cols])

    back.run(back_part, lambda total, h: total.astype(BF16), pick_a[...], pick_b[...])
    joined = list(back.parts())
    for k in range(types * units // step):
        cols = slice(k * step, (k + 1) * step)
        grad = 0.0
        for h in range(HALVES):
            for g in range(YS):
                at = g * share + h * half
                grad = grad + dot_nt(back.full[h, g], w2_ref[cols, at : at + half])
        hidden[:, cols] = (grad * slope[:, cols]).astype(BF16)

    def inputs(g):
        part = 0.0
        for t in range(types):
            part = part + dot_nt(hidden[:, t * units : (t + 1) * units], w1_ref[t, span(g, share), :])
        return part

    last.start(inputs)
    for h in range(HALVES):
        last.relay(h)
    for h in range(HALVES):
        total = last.finish(h)
        out_ref[:, h * half : (h + 1) * half] = back.full[h, y].astype(F32) + total
    last.drain()


VM = pl.BlockSpec(memory_space=pltpu.VMEM)
SM = pl.BlockSpec(memory_space=pltpu.SMEM)
DMA = pltpu.SemaphoreType.DMA


def run(lists, slots, x, kinds, do, w1, w2, wq, wkv, counts):
    rows, width = x.shape
    share = width // YS
    half = share // HALVES
    capacity = 2 * rows // PEERS
    blocks = rows // BLOCK_ROWS
    count = blocks * LISTED_COUNT
    lanes = GROUP_HEADS * BLOCK_ROWS
    tile = (HEAD_SIZE, BLOCK_ROWS)
    spread = [
        pltpu.VMEM((HALVES, YS - 1, rows, half), BF16),
        pltpu.VMEM((HALVES, YS - 1, rows, half), BF16),
    ]
    pairs = [DMA((HALVES, YS - 1)), DMA((HALVES, YS - 1))]
    handover = spread + [
        pltpu.VMEM((HALVES, PEERS, capacity, half), BF16),
        pltpu.VMEM((HALVES, PEERS, capacity, half), BF16),
        pltpu.VMEM((HALVES, YS, rows, half), BF16),
    ] + pairs + [DMA((HALVES,)), DMA((HALVES,))] + pairs
    back = [
        pltpu.VMEM((count,) + tile, BF16),
        pltpu.VMEM((ZS, XS * CS - 1) + tile, BF16),
        pltpu.VMEM((ZS - 1, blocks) + tile, BF16),
        pltpu.VMEM((ZS - 1, blocks) + tile, BF16),
        DMA,
        DMA((ZS,)),
        DMA,
        DMA((ZS - 1,)),
    ]
    return pl.pallas_call(
        kernel,
        out_shape=(
            jax.ShapeDtypeStruct((rows, share), F32),
            jax.ShapeDtypeStruct((rows, share), F32),
        ),
        in_specs=[SM, SM] + [VM] * 8,
        out_specs=(VM, VM),
        scratch_shapes=[
            pltpu.VMEM((rows, w2.shape[0]), BF16),
            pltpu.VMEM((rows, w2.shape[0]), F32),
            pltpu.VMEM((PEERS * capacity, rows), BF16),
            pltpu.VMEM((rows, PEERS * capacity), BF16),
            pltpu.VMEM((blocks, HEAD_SIZE, lanes), BF16),
            pltpu.VMEM((blocks, HEAD_SIZE, lanes), BF16),
            pltpu.VMEM((PEERS * blocks, 2 * HEAD_SIZE, BLOCK_ROWS), BF16),
            pltpu.VMEM((LISTED_COUNT * BLOCK_ROWS, lanes), F32),
            pltpu.VMEM((blocks, LISTED_COUNT * BLOCK_ROWS, lanes), BF16),
            pltpu.VMEM((count,) + tile, BF16),
            pltpu.VMEM((blocks, 8, lanes), F32),
            pltpu.VMEM((rows, share), BF16),
            pltpu.VMEM((rows, 2 * HEAD_SIZE), BF16),
            pltpu.VMEM((XS * CS, ZS, 128), jnp.int32),
            pltpu.VMEM((XS * CS - 1, ZS, 128), jnp.int32),
        ]
        + handover
        + handover
        + [DMA, DMA((PEERS,))]
        + [DMA, DMA]
        + back
        + back
        + [
            pltpu.VMEM((HALVES, rows, half), BF16),
            pltpu.VMEM((HALVES, rows, half), BF16),
            pltpu.VMEM((HALVES, 2, rows, half), BF16),
            pltpu.VMEM((HALVES, 2, rows, half), BF16),
            pltpu.VMEM((2, rows // 2, share), F32),
            DMA((HALVES, 2)),
            DMA((HALVES, 2)),
            DMA((HALVES, 2, 2)),
            DMA((HALVES, 2, 2)),
        ],
        compiler_params=pltpu.CompilerParams(
            collective_id=1, has_side_effects=True, vmem_limit_bytes=63 << 20
        ),
        name="step",
    )(
        lists, slots, x, kinds, do, w1, w2, wq, wkv, counts,
    )


def shards(
    elements,
    element_types,
    handover_counts,
    block_lists,
    w_first,
    w_second,
    w_query,
    key_value_weight,
    attention_cotangent,
):
    row_count, width = elements.shape
    types, units = w_second.shape[:2]
    blocks = row_count // BLOCK_ROWS
    slots = blocks * LISTED_COUNT
    owners = block_lists // blocks
    places = (owners // (ZS * CS) * CS + owners % CS) * ZS + owners // CS % ZS
    slot_of = jnp.sum(
        jnp.where(
            places[None] == jnp.arange(slots, dtype=jnp.int32)[:, None, None],
            jnp.arange(slots, dtype=jnp.int32).reshape(1, blocks, LISTED_COUNT),
            0,
        ),
        axis=(1, 2),
        dtype=jnp.int32,
    )
    w2 = w_second.reshape(types * units, width)
    kv_weight = key_value_weight.transpose(1, 2, 0).reshape(2 * HEAD_SIZE, width)
    attended, x_grad = run(
        block_lists, slot_of, elements, element_types[None, :], attention_cotangent, w_first, w2,
        w_query, kv_weight, handover_counts,
    )
    return attended.astype(BF16), x_grad.astype(BF16)


def solution(mesh):
    return jax.shard_map(
        shards,
        mesh=mesh,
        in_specs=(
            P("det", None),
            P("det"),
            P(),
            P("det", None),
            P(None, None, "head"),
            P(None, "head", None),
            P(None, "head"),
            P(None, None, "head"),
            P("det", "head"),
        ),
        out_specs=(P("det", "head"), P("det", "head")),
        check_vma=False,
    )
```

time: 459 us -> 179 us (0.39)
  waiting for transfers between devices: 244 us -> 0 us
  Pallas kernels: 32.8 us -> 173 us
  blocking collectives: 110 us -> 0 us
  matrix products: 31.6 us -> 0 us
  starting transfers between devices: 16.7 us -> 0 us
  between operations: 14.3 us -> 0.64 us
  local copies, waits for them, and re-layouts: 6.5 us -> 0 us
    pallas_call x1, Pallas kernels: 32.8 us -> 173 us  [run(): pl.pallas_call(kernel, out_shape=(jax.ShapeDtypeStruct((rows, share), F32...]
    all_gather x3 -> x0, waiting for transfers between devices: 129 us -> none  [the longest x1 85.2 us: shards(): all_kv = lax.all_gather(keyval, 'det', axis=0, tiled=True)]
    reduce_scatter x3 -> x0, waiting for transfers between devices: 98.4 us -> none  [the longest x1 35.1 us: shards(): mlp = lax.psum_scatter(partial, 'head', scatter_dimension=1, tiled=True)]
    all_gather x1 -> x0, blocking collectives: 81.7 us -> none  [shards(): all_lists = lax.all_gather(flat_list, 'det', axis=0, tiled=False)]
    dot_general x15 -> x0, matrix products: 31.6 us -> none  [the longest x4 13 us: dot_nt(): lax.dot_general(a, b, (((1,), (1,)), ((), ())), preferred_element_type=F32)]
    all_to_all x1 -> x0, blocking collectives: 28 us -> none  [shards(): lax.all_to_all(outbound, 'det', split_axis=0, concat_axis=0, tiled=True)]
    all_to_all x2 -> x0, waiting for transfers between devices: 16.8 us -> none  [the longest x1 16.7 us: shards(): lax.all_to_all(outbound, 'det', split_axis=0, concat_axis=0, tiled=True)]
    all_to_all x2 -> x0, starting transfers between devices: 16.5 us -> none  [the longest x1 10.7 us: shards(): lax.all_to_all(outbound, 'det', split_axis=0, concat_axis=0, tiled=True)]
  transfers between devices with their start and end apart: 8 -> 0, of which waited for: 7 -> 0; matrix products, arithmetic and copies ran while one was open for 1% -> 0% of each run, Pallas kernels for 0% -> 0%
where the time goes in v3:
time: 179 us
  Pallas kernels  173 us (97%)
  other arithmetic  4.86 us (3%)
    pallas_call x1, Pallas kernels, run(): pl.pallas_call(kernel, out_shape=(jax.ShapeDtypeStruct((rows, share), F32...  173 us

profile of v3, /device:TPU:1, one launch (start us, length us, event | category | flops | bytes accessed | tf_op | source)
XLA Modules:
  0.0 178.6 jit_solution(8241175902684587779)
XLA Ops:
  0.6 0.7 fusion.5
  1.3 0.6 select_reduce_fusion.slot_ref
  2.0 173.1 %step.1 = (f32[512,256]{1,0:T(8,128)}, f32[512,256]{1,0:T(8,128)}) custom-call(s32[4,16]{1,0:T(4,128)} %list_ref.1, s32[64]{0:T(128)} %select_reduce_fusion.slot_ref, bf16[512,1024]{1,0:T(8,128)(2,1)} %x_ref.1, s32[1,512]{1,0:T(1,128)} %bitcast.7, bf16[512,256]{1,0:T(8,128)(2,1)} %do_ref.1, bf16[2,1024,512]{2,1,0:T(8,128)(2,1)} %w1_ref.1, ...), custom_call_target="tpu_custom_call" | custom-call | tf_op jit(solution)/shard_map/step/pallas_call | solution.py:657
  175.0 1.8 convert_element_type.6
  176.8 1.8 convert_element_type.7

commit v4 on v3

--- a/solution.py
+++ b/solution.py
@@ -246,19 +246,20 @@
         (self.sent, self.landed, self.out, self.inb, self.full,
          self.ss, self.sr, self.es, self.er, self.js, self.jr) = bufs
 
-    def run(self, part, finish, pack, unpack):
-        rows = self.full.shape[2]
+    def run(self, part, finish, pack, unpack, prepare=None):
         y = lax.axis_index("head")
         own = spread_start(part, self.sent, self.landed, self.ss, self.sr)
+        if prepare is not None:
+            prepare()
         for h in range(HALVES):
             value = finish(spread_sum(own, h, self.sent, self.landed, self.ss, self.sr), h)
-            packed = dot_nn(pack, value).astype(BF16)
+            packed = dot_nn(pack[...], value).astype(BF16)
             self.out[h] = packed.reshape(self.out.shape[1:])
             exchange_start(self.out.at[h], self.inb.at[h], self.es.at[h], self.er.at[h])
         for h in range(HALVES):
             exchange_wait(self.out.at[h], self.inb.at[h], self.es.at[h], self.er.at[h])
             slots = self.inb[h].reshape(-1, self.inb.shape[-1])
-            self.full[h, y] = dot_nn(unpack, slots).astype(BF16)
+            self.full[h, y] = dot_nn(unpack[...], slots).astype(BF16)
             join_start(self.full.at[h], self.js.at[h], self.jr.at[h])
 
     def parts(self):
@@ -413,9 +414,10 @@
 
 
 def kernel(
-    list_ref, slot_ref, x_ref, kind_ref, do_ref, w1_ref, w2_ref, wq_ref, wkv_ref,
+    list_ref, slot_ref, x_in, kind_ref, do_in, w1_in, w2_in, wq_in, wkv_in,
     count_ref,
     att_ref, out_ref,
+    x_ref, do_ref, w1_ref, w2_ref, wq_ref, wkv_ref, load_sem,
     hidden, slope, pick_a, pick_b, q_t, do_t, kvt, score, prob, glist, stat, dq, kv_grad,
     id_own, id_near,
     *rest,
@@ -442,6 +444,17 @@
     blocks = rows // BLOCK_ROWS
     lanes = GROUP_HEADS * BLOCK_ROWS
     greet()
+    loads = [
+        pltpu.make_async_copy(source, target, load_sem.at[i])
+        for i, (source, target) in enumerate(
+            (
+                (x_in, x_ref), (w1_in, w1_ref), (w2_in, w2_ref),
+                (do_in, do_ref), (wq_in, wq_ref), (wkv_in, wkv_ref),
+            )
+        )
+    ]
+    for load in loads:
+        load.start()
 
     def name(p, carry):
         slot = slot_ref[p]
@@ -456,6 +469,8 @@
     recv_row = slot_rows(counts.T, me, capacity)
     kinds = upright(kind_ref[...])
     step = 256
+    for load in loads[:2]:
+        load.wait()
     for t in range(types):
         for k in range(units // step):
             cols = slice(t * units + k * step, t * units + (k + 1) * step)
@@ -465,11 +480,15 @@
             hidden[:, cols] = (act * keep).astype(BF16)
             slope[:, cols] = pull(jnp.ones_like(pre))[0] * keep
     greeted()
+    for load in loads[2:]:
+        load.wait()
     for j in range(1, XS * CS):
         p, to = ret_v.peer(j)
         push(id_own.at[p], id_near.at[j - 1], id_send, id_recv, to)
-    pick_a[...] = pick_rows(upright(send_row), rows)
-    pick_b[...] = pick_slots(recv_row, rows)
+
+    def prepare():
+        pick_a[...] = pick_rows(upright(send_row), rows)
+        pick_b[...] = pick_slots(recv_row, rows)
 
     def finish_there(total, h):
         own = x_ref[:, pl.ds(pl.multiple_of(y * share + h * half, half), half)]
@@ -477,7 +496,7 @@
 
     there.run(
         lambda g: dot_nn(hidden[...], w2_ref[:, span(g, share)]),
-        finish_there, pick_a[...], pick_b[...],
+        finish_there, pick_a, pick_b, prepare,
     )
     for b in range(blocks):
         do_t[b] = head_rows(do_ref[b * BLOCK_ROWS : (b + 1) * BLOCK_ROWS, :].astype(F32)).astype(
@@ -558,7 +577,7 @@
         inverse = stat[b, 0:1, :]
         out_t = acc * inverse
         where = pl.ds(pl.multiple_of(b * BLOCK_ROWS, BLOCK_ROWS), BLOCK_ROWS)
-        att_ref[where, :] = head_columns(out_t)
+        att_ref[where, :] = head_columns(out_t).astype(BF16)
         d = do_t[b]
         delta = jnp.sum(out_t * d.astype(F32), axis=0, keepdims=True)
         acc = jnp.zeros((HEAD_SIZE, lanes), F32)
@@ -594,16 +613,25 @@
         cols = span(g, share)
         return dot_nt(dq[...], wq_ref[cols, :]) + dot_nn(kv_grad[...], wkv_ref[:, cols])
 
-    back.run(back_part, lambda total, h: total.astype(BF16), pick_a[...], pick_b[...])
-    joined = list(back.parts())
-    for k in range(types * units // step):
-        cols = slice(k * step, (k + 1) * step)
-        grad = 0.0
-        for h in range(HALVES):
-            for g in range(YS):
-                at = g * share + h * half
-                grad = grad + dot_nt(back.full[h, g], w2_ref[cols, at : at + half])
-        hidden[:, cols] = (grad * slope[:, cols]).astype(BF16)
+    back.run(back_part, lambda total, h: total.astype(BF16), pick_a, pick_b)
+    seen = 0
+    for h, g in back.parts():
+        seen += 1
+        if seen < (h + 1) * YS:
+            continue
+        for k in range(types * units // step):
+            cols = slice(k * step, (k + 1) * step)
+            kept = (
+                slice(k // 2 * rows, (k // 2 + 1) * rows), slice(k % 2 * step, (k % 2 + 1) * step)
+            )
+            grad = score[kept] if h else 0.0
+            for group in range(YS):
+                at = group * share + h * half
+                grad = grad + dot_nt(back.full[h, group], w2_ref[cols, at : at + half])
+            if h + 1 < HALVES:
+                score[kept] = grad
+            else:
+                hidden[:, cols] = (grad * slope[:, cols]).astype(BF16)
 
     def inputs(g):
         part = 0.0
@@ -616,12 +644,14 @@
         last.relay(h)
     for h in range(HALVES):
         total = last.finish(h)
-        out_ref[:, h * half : (h + 1) * half] = back.full[h, y].astype(F32) + total
+        value = back.full[h, y].astype(F32) + total
+        out_ref[:, h * half : (h + 1) * half] = value.astype(BF16)
     last.drain()
 
 
 VM = pl.BlockSpec(memory_space=pltpu.VMEM)
 SM = pl.BlockSpec(memory_space=pltpu.SMEM)
+HB = pl.BlockSpec(memory_space=pl.ANY)
 DMA = pltpu.SemaphoreType.DMA
 
 
@@ -657,12 +687,14 @@
     return pl.pallas_call(
         kernel,
         out_shape=(
-            jax.ShapeDtypeStruct((rows, share), F32),
-            jax.ShapeDtypeStruct((rows, share), F32),
+            jax.ShapeDtypeStruct((rows, share), BF16),
+            jax.ShapeDtypeStruct((rows, share), BF16),
         ),
-        in_specs=[SM, SM] + [VM] * 8,
+        in_specs=[SM, SM, HB, VM] + [HB] * 5 + [VM],
         out_specs=(VM, VM),
-        scratch_shapes=[
+        scratch_shapes=[pltpu.VMEM(v.shape, BF16) for v in (x, do, w1, w2, wq, wkv)]
+        + [
+            DMA((6,)),
             pltpu.VMEM((rows, w2.shape[0]), BF16),
             pltpu.VMEM((rows, w2.shape[0]), F32),
             pltpu.VMEM((PEERS * capacity, rows), BF16),
@@ -705,6 +737,21 @@
     )
 
 
+def deliver_kernel(a_ref, b_ref, a_out, b_out):
+    a_out[...] = a_ref[...]
+    b_out[...] = b_ref[...]
+
+
+def deliver(a, b):
+    return pl.pallas_call(
+        deliver_kernel,
+        out_shape=tuple(jax.ShapeDtypeStruct(v.shape, v.dtype) for v in (a, b)),
+        in_specs=[VM, VM],
+        out_specs=(VM, VM),
+        name="deliver",
+    )(a, b)
+
+
 def shards(
     elements,
     element_types,
@@ -737,7 +784,7 @@
         block_lists, slot_of, elements, element_types[None, :], attention_cotangent, w_first, w2,
         w_query, kv_weight, handover_counts,
     )
-    return attended.astype(BF16), x_grad.astype(BF16)
+    return deliver(attended, x_grad)
 
 
 def solution(mesh):

time: 179 us -> 172 us (0.961)
  other arithmetic: 4.86 us -> 1.32 us
  Pallas kernels: 173 us -> 170 us
    convert_element_type x2 -> x0, other arithmetic: 3.54 us -> none  [shards(): return (attended.astype(BF16), x_grad.astype(BF16))]
    pallas_call x1 -> x2, Pallas kernels: 173 us -> 170 us  [the longest x1 168 us: run(): pl.pallas_call(kernel, out_shape=(jax.ShapeDtypeStruct((rows, share), BF1...]
where the time goes in v4:
time: 172 us
  Pallas kernels  170 us (99%)
    pallas_call x1, Pallas kernels, run(): pl.pallas_call(kernel, out_shape=(jax.ShapeDtypeStruct((rows, share), BF1...  168 us

profile of v4, /device:TPU:1, one launch (start us, length us, event | category | flops | bytes accessed | tf_op | source)
XLA Modules:
  0.0 171.6 jit_solution(18331468049760043799)
XLA Ops:
  0.6 0.7 fusion.5
  1.3 0.6 select_reduce_fusion.slot_ref
  2.0 167.8 %step.1 = (bf16[512,256]{1,0:T(8,128)(2,1)}, bf16[512,256]{1,0:T(8,128)(2,1)}) custom-call(s32[4,16]{1,0:T(4,128)} %list_ref.1, s32[64]{0:T(128)} %select_reduce_fusion.slot_ref, bf16[512,1024]{1,0:T(8,128)(2,1)} %x_in.1, s32[1,512]{1,0:T(1,128)} %bitcast.7, bf16[512,256]{1,0:T(8,128)(2,1)} %do_in.1, bf16[2,1024,512]{2,1,0:T(8,128)(2,1)} %w1_in.1, ...), custom_call_target="tpu_custom_call" | custom-call | tf_op jit(solution)/shard_map/step/pallas_call | solution.py:687
  169.8 1.8 %deliver.1 = (bf16[512,256]{1,0:T(8,128)(2,1)}, bf16[512,256]{1,0:T(8,128)(2,1)}) custom-call(bf16[512,256]{1,0:T(8,128)(2,1)} %get-tuple-element.4.a_ref, bf16[512,256]{1,0:T(8,128)(2,1)} %get-tuple-element.5.b_ref), custom_call_target="tpu_custom_call" | custom-call | tf_op jit(solution)/shard_map/deliver/pallas_call | solution.py:746

commit v5 on v4

--- a/solution.py
+++ b/solution.py
@@ -604,6 +604,13 @@
     kv_grad[:, HEAD_SIZE:] = total.T.astype(BF16)
     for i in range(4, ZS - 1):
         ret_k.combine(i)
+
+    def kept_rows(g):
+        return span(g, rows)
+
+    for g in range(YS):
+        cols = slice(g * share, (g + 1) * share)
+        score[g * rows : (g + 1) * rows, :share] = dot_nt(dq[...], wq_ref[cols, :])
     pick_a[...] = pick_rows(upright(recv_row), rows)
     pick_b[...] = pick_slots(send_row, rows)
     total = ret_k.finish(ret_k.combine(ZS - 1))
@@ -611,7 +618,7 @@
 
     def back_part(g):
         cols = span(g, share)
-        return dot_nt(dq[...], wq_ref[cols, :]) + dot_nn(kv_grad[...], wkv_ref[:, cols])
+        return score[kept_rows(g), :share] + dot_nn(kv_grad[...], wkv_ref[:, cols])
 
     back.run(back_part, lambda total, h: total.astype(BF16), pick_a, pick_b)
     seen = 0
@@ -746,8 +753,9 @@
     return pl.pallas_call(
         deliver_kernel,
         out_shape=tuple(jax.ShapeDtypeStruct(v.shape, v.dtype) for v in (a, b)),
-        in_specs=[VM, VM],
-        out_specs=(VM, VM),
+        grid=(2,),
+        in_specs=[pl.BlockSpec((a.shape[0] // 2, a.shape[1]), lambda i: (i, 0))] * 2,
+        out_specs=(pl.BlockSpec((a.shape[0] // 2, a.shape[1]), lambda i: (i, 0)),) * 2,
         name="deliver",
     )(a, b)
 
@@ -767,11 +775,12 @@
     types, units = w_second.shape[:2]
     blocks = row_count // BLOCK_ROWS
     slots = blocks * LISTED_COUNT
-    owners = block_lists // blocks
-    places = (owners // (ZS * CS) * CS + owners % CS) * ZS + owners // CS % ZS
+    spot = jnp.arange(slots, dtype=jnp.int32)[:, None, None]
+    owner = (spot // ZS // CS * ZS + spot % ZS) * CS + spot // ZS % CS
+    listed = block_lists[None]
     slot_of = jnp.sum(
         jnp.where(
-            places[None] == jnp.arange(slots, dtype=jnp.int32)[:, None, None],
+            (listed >= owner * blocks) & (listed < (owner + 1) * blocks),
             jnp.arange(slots, dtype=jnp.int32).reshape(1, blocks, LISTED_COUNT),
             0,
         ),

time: 172 us -> 172 us (level)
  no operation moved by 1% of the time
where the time goes in v5:
time: 172 us
  Pallas kernels  170 us (99%)
    pallas_call x1, Pallas kernels, run(): pl.pallas_call(kernel, out_shape=(jax.ShapeDtypeStruct((rows, share), BF1...  168 us

profile of v5, /device:TPU:1, one launch (start us, length us, event | category | flops | bytes accessed | tf_op | source)
XLA Modules:
  0.0 172.3 jit_solution(4385884439166448010)
XLA Ops:
  0.7 1.3 select_reduce_fusion.slot_ref
  2.0 168.5 %step.1 = (bf16[512,256]{1,0:T(8,128)(2,1)}, bf16[512,256]{1,0:T(8,128)(2,1)}) custom-call(s32[4,16]{1,0:T(4,128)} %list_ref.1, s32[64]{0:T(128)} %select_reduce_fusion.slot_ref, bf16[512,1024]{1,0:T(8,128)(2,1)} %x_in.1, s32[1,512]{1,0:T(1,128)} %bitcast.7, bf16[512,256]{1,0:T(8,128)(2,1)} %do_in.1, bf16[2,1024,512]{2,1,0:T(8,128)(2,1)} %w1_in.1, ...), custom_call_target="tpu_custom_call" | custom-call | tf_op jit(solution)/shard_map/step/pallas_call | solution.py:694
  170.5 1.8 %deliver.1 = (bf16[512,256]{1,0:T(8,128)(2,1)}, bf16[512,256]{1,0:T(8,128)(2,1)}) custom-call(bf16[512,256]{1,0:T(8,128)(2,1)} %get-tuple-element.4.a_ref, bf16[512,256]{1,0:T(8,128)(2,1)} %get-tuple-element.5.b_ref), custom_call_target="tpu_custom_call" | custom-call | tf_op jit(solution)/shard_map/deliver/pallas_call | solution.py:753
  (2 shorter events, 0.0 us)
